TPU v7x, 256 devices: a whole 4x4x8 slice. The times are simulated.
256 devices in a mesh: ctx: 16 (over y, x_lo, core), ch: 16 (over z, x_hi).
Axes of the slice: x: 4 (x_hi: 2, x_lo: 2; x = x_hi * 2 + x_lo), y: 4, z: 8, core: 2. Of those that a mesh axis runs over, the one named last changes fastest.
Arguments:
- hidden_in: bfloat16 [16384, 4096], P('ctx', 'ch'), may hold values from -6 to 6
- in_weight: bfloat16 [3, 4096, 4096], P(None, None, 'ch'), may hold values from -0.09375 to 0.09375
- out_weight: bfloat16 [4096, 4096], P('ch'), may hold values from -0.125 to 0.125
- decay: float32 [4096, 16], P('ch'), may hold values from 1.5258789e-05 to 0.0061035156
- residue: float32 [4096, 16], P('ch'), may hold values from -0.0234375 to 0.0234375
- skip_gain: float32 [4096], P('ch'), may hold values from -4 to 4
- block_order: int32 [32], replicated, may hold values from 0 to 31, each once
Outputs:
- layer_out: bfloat16 [16384, 4096], P('ctx', 'ch')
Inputs may be any that keep to these rules, and one draw needn't show every extreme that they name: `block_order`: every half-block of the sequence stands in exactly one slot.
All inputs are finite; a program needn't handle non-finite values.
Results may differ from a plain program's by a relative error of at most 0.012.
Values may be sent and summed in bfloat16 or wider, within the bound.
No kernel may reach another device: no remote copies, remote signals or barrier semaphores. Data moves between devices by JAX's collectives and lax.ppermute only.
A program may use at most 128 MiB of HBM per device.

v0:
```python
import jax
import jax.numpy as jnp
from jax import lax
from jax.experimental import pallas as pl
from jax.experimental.pallas import tpu as pltpu
from jax.sharding import Mesh
from jax.sharding import PartitionSpec as P

F32 = jnp.float32
BF16 = jnp.bfloat16
SWAP = [(0, 1), (1, 0)]
ORDER = 16
SEGS = 8
HBM = pl.BlockSpec(memory_space=pltpu.HBM)
SMEM = pl.BlockSpec(memory_space=pltpu.SMEM)
VMEM = pl.BlockSpec()


def around(size, step):
    return [(i, (i + step) % size) for i in range(size)]


GROUP = 4


def project_all(where, *refs, n_chunks):
    chunks = refs[:n_chunks]
    parts, (own, rates, mixed, ends, state, query) = refs[n_chunks : n_chunks + 2], refs[n_chunks + 2 : n_chunks + 8]
    rows, own_rows, peer_rows, own_sums, peer_sums, mixed_rows, sems = refs[n_chunks + 8 :]
    tokens, width = chunks[0].shape
    steps = tokens // SEGS
    for i, chunk in enumerate(chunks):
        pltpu.make_async_copy(chunk, rows.at[where[i]], sems.at[i]).start()
        block = pl.ds(pl.multiple_of(where[i] * width, width), width)
        for k, j in enumerate((1, 2, 0)):
            target = own_rows.at[i, :, pl.ds(k * width, width)]
            pltpu.make_async_copy(own.at[j, block, :], target, sems.at[n_chunks + i]).start()
    for p, part in enumerate(parts):
        blocks = pl.ds(pl.multiple_of(where[n_chunks + p], part.shape[1]), part.shape[1])
        for k in range(part.shape[0]):
            target = peer_rows.at[blocks, :, pl.ds(k * width, width)]
            pltpu.make_async_copy(part.at[k], target, sems.at[2 * n_chunks]).start()

    def own_step(g, _):
        total = None
        for j in range(GROUP):
            i = GROUP * g + j
            pltpu.make_async_copy(rows.at[0], rows.at[0], sems.at[i]).wait()
            pltpu.make_async_copy(own_rows.at[0], own_rows.at[0], sems.at[n_chunks + i]).wait()
            term = jnp.dot(rows[where[i]], own_rows[i], preferred_element_type=F32)
            total = term if total is None else total + term
        own_sums[...] += total
        return 0

    def peer_step(g, _):
        total = None
        for j in range(GROUP):
            term = jnp.dot(rows[GROUP * g + j], peer_rows[GROUP * g + j], preferred_element_type=F32)
            total = term if total is None else total + term
        peer_sums[...] += total
        return 0

    own_sums[...] = jnp.zeros(own_sums.shape, F32)
    peer_sums[...] = jnp.zeros(peer_sums.shape, F32)
    lax.fori_loop(0, n_chunks // GROUP, own_step, 0)
    pltpu.make_async_copy(peer_rows, peer_rows, sems.at[2 * n_chunks]).wait()
    lax.fori_loop(0, n_chunks // GROUP, peer_step, 0)
    for half, sums in enumerate((own_sums, peer_sums)):
        keys, values = sums[:, :width].astype(BF16), sums[:, width : 2 * width].astype(BF16)
        product = (keys.astype(F32) * values.astype(F32)).astype(BF16)
        place = slice(half * width, (half + 1) * width)
        mixed[:, place] = product
        for g in range(width // 128):
            mixed_rows[half * width // 128 + g] = product[:, g * 128 : (g + 1) * 128].astype(F32)
    query[...] = own_sums[:, 2 * width :].astype(BF16)
    fall = jnp.exp(-rates[...])
    later = (SEGS - 1 - lax.broadcasted_iota(jnp.int32, (SEGS, 128), 0)).astype(F32) * float(steps)
    for g in range(2 * width // 128):
        lanes = slice(g * 128, (g + 1) * 128)
        falls = [jnp.broadcast_to(fall[n : n + 1, lanes], (SEGS, 128)) for n in range(ORDER)]

        def step(t, states, g=g, falls=falls):
            now = mixed_rows[g, pl.ds(t, SEGS, stride=steps), :]
            return tuple(f * s + now for f, s in zip(falls, states))

        states = lax.fori_loop(
            0, steps, step, tuple(jnp.zeros((SEGS, 128), F32) for _ in range(ORDER)), unroll=4
        )
        for n in range(ORDER):
            ends[n, :, lanes] = states[n]
            weight = jnp.exp(-rates[n : n + 1, lanes] * later)
            state[n : n + 1, lanes] = jnp.sum(weight * states[n], axis=0, keepdims=True)


def project_query(where, *refs, n_chunks):
    chunks, parts = refs[:n_chunks], refs[n_chunks : n_chunks + 2]
    query, rows, weight_rows, sems = refs[n_chunks + 2 :]
    for p, part in enumerate(parts):
        blocks = pl.ds(pl.multiple_of(where[n_chunks + p], part.shape[1]), part.shape[1])
        pltpu.make_async_copy(part.at[0], weight_rows.at[blocks], sems.at[n_chunks]).start()
    for i, chunk in enumerate(chunks):
        pltpu.make_async_copy(chunk, rows.at[i], sems.at[i]).start()
    pltpu.make_async_copy(weight_rows, weight_rows, sems.at[n_chunks]).wait()
    total = jnp.zeros(query.shape, F32)
    for g in range(0, n_chunks, GROUP):
        for i in range(g, g + GROUP):
            pltpu.make_async_copy(rows.at[i], rows.at[i], sems.at[i]).wait()
        for i in range(g, g + GROUP):
            total += jnp.dot(rows[i], weight_rows[where[i]], preferred_element_type=F32)
    query[...] = total.astype(BF16)


def pass_on(lags, *refs, n_pieces):
    pieces, rates, outs = refs[:n_pieces], refs[n_pieces], refs[n_pieces + 1 :]
    rate = -rates[...]
    per_piece = pieces[0].shape[0]
    for k, out in enumerate(outs):
        total = jnp.zeros(rate.shape, F32)
        for p, piece in enumerate(pieces):
            for i in range(per_piece):
                lag = lags[(k * n_pieces + p) * per_piece + i]
                live = (lag >= 0.0).astype(F32)
                total = total + live * (jnp.exp(rate * jnp.maximum(lag, 0.0)) * piece[i])
        out[...] = total


def convolve_and_project(where, *refs, n_given, n_parts, n_outs):
    given = refs[:n_given]
    ends, mixed, query_own, query_peer, rates, gains, skip, out_own = refs[n_given : n_given + 8]
    parts = refs[n_given + 8 : n_given + 8 + n_parts]
    outs = refs[n_given + 8 + n_parts : n_given + 8 + n_parts + n_outs]
    mixed_rows, conv_rows, gated, own_cols, peer_cols, stage, sems = refs[n_given + 8 + n_parts + n_outs :]
    tokens, width = mixed.shape
    half = width // 2
    steps = tokens // SEGS
    cols = outs[0].shape[1]
    deep = parts[0].shape[1]
    pltpu.make_async_copy(out_own, own_cols, sems.at[0]).start()
    for i, part in enumerate(parts):
        target = peer_cols.at[:, pl.ds(pl.multiple_of(where[i] * deep, deep), deep)]
        pltpu.make_async_copy(part, target, sems.at[1]).start()
    for g in range(width // 128):
        mixed_rows[g] = mixed[:, g * 128 : (g + 1) * 128].astype(F32)
    incoming = given[0][...]
    for more in given[1:]:
        incoming = incoming + more[...]
    rate = rates[...]
    fall = jnp.exp(-rate)
    gain = gains[...]
    order = lax.broadcasted_iota(jnp.int32, (SEGS, 128), 0)
    before = order.astype(F32) * float(steps)
    for g in range(width // 128):
        lanes = slice(g * 128, (g + 1) * 128)
        starts = []
        for n in range(ORDER):
            total = ends[n, :, lanes]
            slow = rate[n : n + 1, lanes]
            for reach in (1, 2, 4):
                moved = jnp.where(order >= reach, pltpu.roll(total, reach, 0), 0.0)
                total = total + jnp.exp(-slow * float(reach * steps)) * moved
            total = jnp.where(order >= 1, pltpu.roll(total, 1, 0), 0.0)
            starts.append(total + jnp.exp(-slow * before) * incoming[n : n + 1, lanes])
        falls = [jnp.broadcast_to(fall[n : n + 1, lanes], (SEGS, 128)) for n in range(ORDER)]
        rises = [jnp.broadcast_to(gain[n : n + 1, lanes], (SEGS, 128)) for n in range(ORDER)]

        def step(t, states, g=g, falls=falls, rises=rises):
            now = mixed_rows[g, pl.ds(t, SEGS, stride=steps), :]
            states = tuple(f * s + now for f, s in zip(falls, states))
            terms = [r * s for r, s in zip(rises, states)]
            while len(terms) > 1:
                terms = [a + b for a, b in zip(terms[::2], terms[1::2])]
            conv_rows[g, pl.ds(t, SEGS, stride=steps), :] = terms[0]
            return states

        lax.fori_loop(0, steps, step, tuple(starts), unroll=2)
        inner = conv_rows[g] + skip[:, lanes] * mixed_rows[g]
        query = (query_own, query_peer)[g * 128 // half]
        gated[:, lanes] = (query[:, g * 128 % half : g * 128 % half + 128].astype(F32) * inner).astype(BF16)
    pltpu.make_async_copy(own_cols, own_cols, sems.at[0]).wait()
    pltpu.make_async_copy(peer_cols, peer_cols, sems.at[1]).wait()

    def block(i, _):
        k = where[len(parts) + i]
        place = pl.multiple_of(k * cols, cols)
        own = jnp.dot(gated[:, :half], own_cols[:, pl.ds(place, cols)], preferred_element_type=F32)
        peer = jnp.dot(gated[:, half:], peer_cols[:, pl.ds(place, cols)], preferred_element_type=F32)
        stage[i] = (own + peer).astype(BF16)
        return 0

    copies = []
    for first in (0, 4):
        lax.fori_loop(first, first + 4, block, 0)
        for i in range(first, first + 4):
            for out, rows in ((outs[0], pl.ds(0, tokens // 2)), (outs[1], pl.ds(tokens // 2, tokens // 2))):
                if i > 0:
                    out, rows = outs[i + 1], pl.ds(0, tokens)
                if i == 0 or len(copies) < i + 2:
                    copies.append(pltpu.make_async_copy(stage.at[i, rows, :], out, sems.at[2 + len(copies)]))
                    copies[-1].start()
    for copy in copies:
        copy.wait()


def per_device(hidden_in, in_weight, out_weight, decay, residue, skip_gain, block_order):
    y, xl, core = lax.axis_index("y"), lax.axis_index("xl"), lax.axis_index("core")
    z, xh = lax.axis_index("z"), lax.axis_index("xh")
    n_y, n_z = lax.axis_size("y"), lax.axis_size("z")
    tok_rows, width = hidden_in.shape
    features = in_weight.shape[1]
    tokens = tok_rows // 2

    mine = lax.dynamic_slice_in_dim(hidden_in, xh * tokens, tokens, 0)
    others = lax.dynamic_slice_in_dim(hidden_in, (1 - xh) * tokens, tokens, 0)
    small = jnp.concatenate([decay.T, residue.T, skip_gain[None]], 0)
    out_cols = features // n_z

    def swap(piece, axis="xh"):
        return lax.ppermute(piece, axis, SWAP)

    together = lax.optimization_barrier

    def ahead_z(x):
        return lax.ppermute(x, "z", around(n_z, 1))

    def back_z(x):
        return lax.ppermute(x, "z", around(n_z, -1))

    half, blocks = features // 2, features // 2 // width
    at = core * half
    mixed_part = lax.dynamic_slice(in_weight, (1, at, 0), (2, half, width)).reshape(2, blocks, width, width)
    of1, ob1, p0, small_peer, mixed_part = together(
        (ahead_z(mine), back_z(mine), swap(others), swap(small), mixed_part)
    )
    mixed_part = swap(mixed_part)
    of2, ob2, pf1, pb1 = together((ahead_z(of1), back_z(ob1), ahead_z(p0), back_z(p0)))
    of3, ob3, pf2, pb2 = together((ahead_z(of2), back_z(ob2), ahead_z(pf1), back_z(pb1)))
    of4, pf3, pb3, at = together((ahead_z(of3), ahead_z(pf2), back_z(pb2), at))
    query_part = lax.dynamic_slice(in_weight, (0, at, 0), (1, half, width)).reshape(1, blocks, width, width)
    pb4, mixed_part, query_part, at = together((back_z(pb3), mixed_part, query_part, at))
    query_part = swap(query_part)
    in_parts = [mixed_part, swap(mixed_part, "core")]
    out_part = lax.dynamic_slice_in_dim(out_weight, at, half, 1)
    small = jnp.concatenate([small, small_peer], 1)
    rates, gains, skip = small[:ORDER], small[ORDER : 2 * ORDER], small[2 * ORDER :]
    chunks = [mine, of1, of2, of3, of4, ob1, ob2, ob3, p0, pf1, pf2, pf3, pb1, pb2, pb3, pb4]
    chunk_at = [((z + o) % n_z) * 2 + xh for o in (0, -1, -2, -3, -4, 1, 2, 3)]
    chunk_at += [((z + o) % n_z) * 2 + 1 - xh for o in (0, -1, -2, -3, 1, 2, 3, 4)]
    part_at = [core * blocks, (1 - core) * blocks]
    where = jnp.stack(chunk_at + part_at).astype(jnp.int32)
    reach = [4, -3, 3, 2, -2, 1, -1, 0]
    where_out = jnp.stack([core, 1 - core] + [(z + r) % n_z for r in reach]).astype(jnp.int32)

    params = pltpu.CompilerParams(vmem_limit_bytes=60 << 20)
    mixed, ends, state, query_own = pl.pallas_call(
        lambda *refs: project_all(*refs, n_chunks=len(chunks)),
        in_specs=[SMEM] + [HBM] * (len(chunks) + 3) + [VMEM],
        out_specs=[VMEM] * 4,
        out_shape=[
            jax.ShapeDtypeStruct((tokens, 2 * width), BF16),
            jax.ShapeDtypeStruct((ORDER, SEGS, 2 * width), F32),
            jax.ShapeDtypeStruct((ORDER, 2 * width), F32),
            jax.ShapeDtypeStruct((tokens, width), BF16),
        ],
        scratch_shapes=[
            pltpu.VMEM((len(chunks), tokens, width), BF16),
            pltpu.VMEM((len(chunks), width, 3 * width), BF16),
            pltpu.VMEM((len(chunks), width, 2 * width), BF16),
            pltpu.VMEM((tokens, 3 * width), F32),
            pltpu.VMEM((tokens, 2 * width), F32),
            pltpu.VMEM((2 * width // 128, tokens, 128), F32),
            pltpu.SemaphoreType.DMA((2 * len(chunks) + 1,)),
        ],
        compiler_params=params,
    )(where, *chunks, *in_parts, in_weight, rates)

    pair = jnp.stack([state, lax.ppermute(state, "core", SWAP)])
    turned = jnp.concatenate([pair[:, :, width:], pair[:, :, :width]], 2)
    pieces = [
        pair,
        lax.ppermute(pair, "xl", SWAP),
        lax.ppermute(turned, "xh", SWAP),
        lax.ppermute(turned, ("xl", "xh"), [(0, 3), (3, 0), (1, 2), (2, 1)]),
    ]
    query_part, out_part, pieces = together((query_part, out_part, pieces))
    out_part = swap(out_part)
    query_peer = pl.pallas_call(
        lambda *refs: project_query(*refs, n_chunks=len(chunks)),
        in_specs=[SMEM] + [HBM] * (len(chunks) + 2),
        out_specs=VMEM,
        out_shape=jax.ShapeDtypeStruct((tokens, width), BF16),
        scratch_shapes=[
            pltpu.VMEM((len(chunks), tokens, width), BF16),
            pltpu.VMEM((len(chunks), width, width), BF16),
            pltpu.SemaphoreType.DMA((len(chunks) + 1,)),
        ],
        compiler_params=params,
    )(where, *chunks, query_part, swap(query_part, "core"))
    slots = jnp.stack(
        [
            8 * y + 4 * (xl ^ dl) + 2 * (core ^ dc) + (xh ^ dh)
            for dl, dh in ((0, 0), (1, 0), (0, 1), (1, 1))
            for dc in (0, 1)
        ]
    )
    ahead = [0, 1, -1, 2]
    targets = jnp.stack([8 * ((y + o) % n_y) + 4 * xl + 2 * core + xh for o in ahead])
    names = jnp.arange(block_order.shape[0])

    def place_of(which):
        return jnp.sum(jnp.where(names[None] == which[:, None], block_order[None], 0), axis=1)

    lags = ((place_of(targets)[:, None] - 1 - place_of(slots)[None]) * tokens).astype(F32).reshape(-1)
    given = pl.pallas_call(
        lambda *refs: pass_on(*refs, n_pieces=len(pieces)),
        in_specs=[SMEM] + [VMEM] * (len(pieces) + 1),
        out_specs=[VMEM] * len(ahead),
        out_shape=[jax.ShapeDtypeStruct(state.shape, F32)] * len(ahead),
    )(lags, *pieces, rates)
    given = [given[0]] + [lax.ppermute(g, "y", around(n_y, o)) for g, o in zip(given[1:], ahead[1:])]

    out_part, given, query_peer = together((out_part, given, query_peer))
    out_parts = [out_part, swap(out_part, "core")]
    n_outs = len(reach) + 1
    full = jax.ShapeDtypeStruct((tokens, out_cols), BF16)
    half_rows = jax.ShapeDtypeStruct((tokens // 2, out_cols), BF16)
    outs = pl.pallas_call(
        lambda *refs: convolve_and_project(*refs, n_given=len(given), n_parts=len(out_parts), n_outs=n_outs),
        in_specs=[SMEM] + [VMEM] * (len(given) + 7) + [HBM] * (1 + len(out_parts)),
        out_specs=[HBM] * n_outs,
        out_shape=[half_rows] * 2 + [full] * (n_outs - 2),
        scratch_shapes=[
            pltpu.VMEM((2 * width // 128, tokens, 128), F32),
            pltpu.VMEM((2 * width // 128, tokens, 128), F32),
            pltpu.VMEM((tokens, 2 * width), BF16),
            pltpu.VMEM(out_weight.shape, BF16),
            pltpu.VMEM(out_weight.shape, BF16),
            pltpu.VMEM((len(reach), tokens, out_cols), BF16),
            pltpu.SemaphoreType.DMA((2 + n_outs,)),
        ],
        compiler_params=params,
    )(
        where_out,
        *given,
        ends,
        mixed,
        query_own,
        query_peer,
        rates,
        gains,
        skip,
        out_weight,
        *out_parts,
    )
    share = dict(zip(reach[1:], outs[2:]))
    low, high = slice(0, tokens // 2), slice(tokens // 2, tokens)

    def add(a, b):
        return (a.astype(F32) + b.astype(F32)).astype(BF16)

    forward = jnp.concatenate([add(ahead_z(outs[0]), share[3][low]), share[3][high]], 0)
    backward = jnp.concatenate([share[-3][low], add(back_z(outs[1]), share[-3][high])], 0)
    for hop in (2, 1):
        forward = add(ahead_z(forward), share[hop])
        backward = add(back_z(backward), share[-hop])
    total = ahead_z(forward).astype(F32) + back_z(backward).astype(F32) + share[0].astype(F32)
    total = total.astype(BF16)
    keep = lax.dynamic_slice_in_dim(total, xh * width, width, 1)
    take = swap(lax.dynamic_slice_in_dim(total, (1 - xh) * width, width, 1))
    first = xh == 0
    return jnp.concatenate([jnp.where(first, keep, take), jnp.where(first, take, keep)], 0)


def solution(mesh):
    ctx, ch = ("y", "xl", "core"), ("z", "xh")
    grid = Mesh(mesh.devices.reshape(4, 2, 2, 8, 2), ctx + ch)
    placed = (
        P(ctx, ch),
        P(None, None, ch),
        P(ch, None),
        P(ch, None),
        P(ch, None),
        P(ch),
        P(),
    )
    return jax.shard_map(
        per_device, mesh=grid, in_specs=placed, out_specs=P(ctx, ch), check_vma=False
    )
```

profile of v0, /device:TPU:8, one launch (start us, length us, event | category | flops | bytes accessed | tf_op | source)
XLA Modules:
  0.0 200.0 jit_solution(12988719456550969854)
XLA Ops:
  3.1 4.0 %collective-permute-start.1 = (bf16[512,256]{1,0:T(8,128)(2,1)S(1)}, bf16[512,256]{1,0:T(8,128)(2,1)S(1)}, u32[]{:S(2)}, u32[]{:S(2)}) collective-permute-start(bf16[512,256]{1,0:T(8,128)(2,1)S(1)} %get-tuple-element.108.refs_1_), channel_id=1, source_target_pairs={{0,14},{2,0},{4,2},{6,4},{8,6},{10,8},{12,10},{14,12},{1,15},{3,1}... | collective-permute-start | bytes 786440 | tf_op jit(solution)/shard_map/ppermute | solution.py:226
  7.1 3.0 %collective-permute-start.2 = (bf16[512,256]{1,0:T(8,128)(2,1)S(1)}, bf16[512,256]{1,0:T(8,128)(2,1)S(1)}, u32[]{:S(2)}, u32[]{:S(2)}) collective-permute-start(bf16[512,256]{1,0:T(8,128)(2,1)S(1)} %get-tuple-element.107), channel_id=1, source_target_pairs={{0,1},{1,0},{2,3},{3,2},{4,5},{5,4},{6,7},{7,6},{8,9},{9,8},{10,11... | collective-permute-start | bytes 786440 | tf_op jit(solution)/shard_map/ppermute | solution.py:218
  13.2 4.1 %collective-permute-done.3 = f32[33,256]{1,0:T(8,128)S(1)} collective-permute-done((f32[33,256]{1,0:T(8,128)S(1)}, f32[33,256]{1,0:T(8,128)S(1)}, u32[]{:S(2)}, u32[]{:S(2)}) %collective-permute-start.3) | collective-permute-done | bytes 33824 | tf_op jit(solution)/shard_map/ppermute | solution.py:218
  17.3 3.1 %collective-permute-start.16 = (bf16[2,8,256,256]{3,2,1,0:T(8,128)(2,1)S(1)}, bf16[2,8,256,256]{3,2,1,0:T(8,128)(2,1)}, u32[]{:S(2)}, u32[]{:S(2)}) collective-permute-start(bf16[2,8,256,256]{3,2,1,0:T(8,128)(2,1)S(1)} %bitcast.47), channel_id=1, source_target_pairs={{0,1},{1,0},{2,3},{3,2},{4,5},{5,4},{6,7},{7,6},{8,9},{9,8},{10,11... | collective-permute-start | bytes 6291464 | tf_op jit(solution)/shard_map/ppermute | solution.py:218
  20.4 3.2 %collective-permute-start.5 = (bf16[512,256]{1,0:T(8,128)(2,1)S(1)}, bf16[512,256]{1,0:T(8,128)(2,1)S(1)}, u32[]{:S(2)}, u32[]{:S(2)}) collective-permute-start(bf16[512,256]{1,0:T(8,128)(2,1)S(1)} %collective-permute-done.1.refs_6_), channel_id=1, source_target_pairs={{0,14},{2,0},{4,2},{6,4},{8,6},{10,8},{12,10},{14,12},{1,15},{3,1}... | collective-permute-start | bytes 786440 | tf_op jit(solution)/shard_map/ppermute | solution.py:226
  23.6 3.2 %collective-permute-start.7 = (bf16[512,256]{1,0:T(8,128)(2,1)S(1)}, bf16[512,256]{1,0:T(8,128)(2,1)S(1)}, u32[]{:S(2)}, u32[]{:S(2)}) collective-permute-start(bf16[512,256]{1,0:T(8,128)(2,1)S(1)} %collective-permute-done.2.refs_9_), channel_id=1, source_target_pairs={{0,14},{2,0},{4,2},{6,4},{8,6},{10,8},{12,10},{14,12},{1,15},{3,1}... | collective-permute-start | bytes 786440 | tf_op jit(solution)/shard_map/ppermute | solution.py:226
  26.9 4.0 %collective-permute-done.4.refs_3_ = bf16[512,256]{1,0:T(8,128)(2,1)S(1)} collective-permute-done((bf16[512,256]{1,0:T(8,128)(2,1)S(1)}, bf16[512,256]{1,0:T(8,128)(2,1)S(1)}, u32[]{:S(2)}, u32[]{:S(2)}) %collective-permute-start.4) | collective-permute-done | bytes 262176 | tf_op jit(solution)/shard_map/ppermute | solution.py:223
  33.9 3.2 %collective-permute-start.11 = (bf16[512,256]{1,0:T(8,128)(2,1)S(1)}, bf16[512,256]{1,0:T(8,128)(2,1)S(1)}, u32[]{:S(2)}, u32[]{:S(2)}) collective-permute-start(bf16[512,256]{1,0:T(8,128)(2,1)S(1)} %collective-permute-done.7.refs_13_), channel_id=1, source_target_pairs={{0,14},{2,0},{4,2},{6,4},{8,6},{10,8},{12,10},{14,12},{1,15},{3,1}... | collective-permute-start | bytes 786440 | tf_op jit(solution)/shard_map/ppermute | solution.py:226
  37.1 3.2 %collective-permute-start.9 = (bf16[512,256]{1,0:T(8,128)(2,1)S(1)}, bf16[512,256]{1,0:T(8,128)(2,1)S(1)}, u32[]{:S(2)}, u32[]{:S(2)}) collective-permute-start(bf16[512,256]{1,0:T(8,128)(2,1)S(1)} %collective-permute-done.5.refs_7_), channel_id=1, source_target_pairs={{0,14},{2,0},{4,2},{6,4},{8,6},{10,8},{12,10},{14,12},{1,15},{3,1}... | collective-permute-start | bytes 786440 | tf_op jit(solution)/shard_map/ppermute | solution.py:226
  40.4 3.3 %collective-permute-done.10.refs_11_ = bf16[512,256]{1,0:T(8,128)(2,1)S(1)} collective-permute-done((bf16[512,256]{1,0:T(8,128)(2,1)S(1)}, bf16[512,256]{1,0:T(8,128)(2,1)S(1)}, u32[]{:S(2)}, u32[]{:S(2)}) %collective-permute-start.10) | collective-permute-done | bytes 262176 | tf_op jit(solution)/shard_map/ppermute | solution.py:223
  51.2 4.4 %collective-permute-done.12.refs_5_ = bf16[512,256]{1,0:T(8,128)(2,1)S(1)} collective-permute-done((bf16[512,256]{1,0:T(8,128)(2,1)S(1)}, bf16[512,256]{1,0:T(8,128)(2,1)S(1)}, u32[]{:S(2)}, u32[]{:S(2)}) %collective-permute-start.12) | collective-permute-done | bytes 262176 | tf_op jit(solution)/shard_map/ppermute | solution.py:223
  71.5 13.9 %shard_map.73 = (bf16[512,512]{1,0:T(8,128)(2,1)}, f32[16,8,512]{2,1,0:T(8,128)}, f32[16,512]{1,0:T(8,128)}, bf16[512,256]{1,0:T(8,128)(2,1)}) custom-call(s32[18]{0:T(128)} %stack.170.refs_0_, bf16[512,256]{1,0:T(8,128)(2,1)} %copy-done.1, bf16[512,256]{1,0:T(8,128)(2,1)} %copy-done.3, bf16[512,256]{1,0:T(8,128)(2,1)} %copy-done.6, ...), custom_call_target="tpu_custom_call" | custom-call | tf_op jit(solution)/shard_map/pallas_call | solution.py:254
  107.3 5.9 %shard_map.75.refs_8_ = bf16[512,256]{1,0:T(8,128)(2,1)} custom-call(s32[18]{0:T(128)} %stack.170.refs_0_, bf16[512,256]{1,0:T(8,128)(2,1)} %copy-done.1, bf16[512,256]{1,0:T(8,128)(2,1)} %copy-done.3, bf16[512,256]{1,0:T(8,128)(2,1)} %copy-done.6, bf16[512,256]{1,0:T(8,128)(2,1)} %copy-done.12, bf16[512,256]{1,0:T(8,128)(2,1)} %copy-done.14, ...), custom_call_target="tpu_custom_call" | custom-call | tf_op jit(solution)/shard_map/pallas_call | solution.py:286
  113.3 10.8 %collective-permute-done.23.refs_13_ = bf16[256,2048]{1,0:T(8,128)(2,1)S(1)} collective-permute-done((bf16[256,2048]{1,0:T(8,128)(2,1)S(1)}, bf16[256,2048]{1,0:T(8,128)(2,1)S(1)}, u32[]{:S(2)}, u32[]{:S(2)}) %collective-permute-start.23) | collective-permute-done | bytes 1048608 | tf_op jit(solution)/shard_map/ppermute | solution.py:218
  127.8 11.3 %shard_map.76 = (bf16[256,512]{1,0:T(8,128)(2,1)}, bf16[256,512]{1,0:T(8,128)(2,1)}, bf16[512,512]{1,0:T(8,128)(2,1)}, bf16[512,512]{1,0:T(8,128)(2,1)}, bf16[51...) custom-call(s32[10]{0:T(128)} %stack.151.refs_0_, ...), custom_call_target="tpu_custom_call" | custom-call | tf_op jit(solution)/shard_map/pallas_call | solution.py:326
  140.2 3.2 %collective-permute-start.33 = (bf16[256,512]{1,0:T(8,128)(2,1)}, bf16[256,512]{1,0:T(8,128)(2,1)S(1)}, u32[]{:S(2)}, u32[]{:S(2)}) collective-permute-start(bf16[256,512]{1,0:T(8,128)(2,1)} %get-tuple-element.101), channel_id=1, source_target_pairs={{0,14},{2,0},{4,2},{6,4},{8,6},{10,8},{12,10},{14,12},{1,15},{3,1}... | collective-permute-start | bytes 786440 | tf_op jit(solution)/shard_map/ppermute | solution.py:226
  144.5 4.5 %collective-permute-done.29 = bf16[256,512]{1,0:T(8,128)(2,1)S(1)} collective-permute-done((bf16[256,512]{1,0:T(8,128)(2,1)}, bf16[256,512]{1,0:T(8,128)(2,1)S(1)}, u32[]{:S(2)}, u32[]{:S(2)}) %collective-permute-start.29) | collective-permute-done | bytes 262176 | tf_op jit(solution)/shard_map/ppermute | solution.py:223
  150.3 3.3 %collective-permute-start.34 = (bf16[512,512]{1,0:T(8,128)(2,1)S(1)}, bf16[512,512]{1,0:T(8,128)(2,1)S(1)}, u32[]{:S(2)}, u32[]{:S(2)}) collective-permute-start(bf16[512,512]{1,0:T(8,128)(2,1)S(1)} %pad_maximum_fusion.1), channel_id=1, source_target_pairs={{0,14},{2,0},{4,2},{6,4},{8,6},{10,8},{12,10},{14,12},{1,15},{3,1}... | collective-permute-start | bytes 1572872 | tf_op jit(solution)/shard_map/ppermute | solution.py:226
  153.5 10.9 %collective-permute-done.30 = bf16[512,512]{1,0:T(8,128)(2,1)S(1)} collective-permute-done((bf16[512,512]{1,0:T(8,128)(2,1)S(1)}, bf16[512,512]{1,0:T(8,128)(2,1)S(1)}, u32[]{:S(2)}, u32[]{:S(2)}) %collective-permute-start.30) | collective-permute-done | bytes 524320 | tf_op jit(solution)/shard_map/ppermute | solution.py:223
  164.9 3.3 %collective-permute-start.35 = (bf16[512,512]{1,0:T(8,128)(2,1)S(1)}, bf16[512,512]{1,0:T(8,128)(2,1)S(1)}, u32[]{:S(2)}, u32[]{:S(2)}) collective-permute-start(bf16[512,512]{1,0:T(8,128)(2,1)S(1)} %add_convert_fusion.2), channel_id=1, source_target_pairs={{0,14},{2,0},{4,2},{6,4},{8,6},{10,8},{12,10},{14,12},{1,15},{3,1}... | collective-permute-start | bytes 1572872 | tf_op jit(solution)/shard_map/ppermute | solution.py:226
  168.1 10.0 %collective-permute-done.31 = bf16[512,512]{1,0:T(8,128)(2,1)S(1)} collective-permute-done((bf16[512,512]{1,0:T(8,128)(2,1)S(1)}, bf16[512,512]{1,0:T(8,128)(2,1)S(1)}, u32[]{:S(2)}, u32[]{:S(2)}) %collective-permute-start.31) | collective-permute-done | bytes 524320 | tf_op jit(solution)/shard_map/ppermute | solution.py:223
  178.5 3.3 %collective-permute-start.36 = (bf16[512,512]{1,0:T(8,128)(2,1)S(1)}, bf16[512,512]{1,0:T(8,128)(2,1)S(1)}, u32[]{:S(2)}, u32[]{:S(2)}) collective-permute-start(bf16[512,512]{1,0:T(8,128)(2,1)S(1)} %add_convert_fusion.1), channel_id=1, source_target_pairs={{0,14},{2,0},{4,2},{6,4},{8,6},{10,8},{12,10},{14,12},{1,15},{3,1}... | collective-permute-start | bytes 1572872 | tf_op jit(solution)/shard_map/ppermute | solution.py:226
  181.8 9.0 %collective-permute-done.32 = bf16[512,512]{1,0:T(8,128)(2,1)S(1)} collective-permute-done((bf16[512,512]{1,0:T(8,128)(2,1)S(1)}, bf16[512,512]{1,0:T(8,128)(2,1)S(1)}, u32[]{:S(2)}, u32[]{:S(2)}) %collective-permute-start.32) | collective-permute-done | bytes 524320 | tf_op jit(solution)/shard_map/ppermute | solution.py:223
  193.1 6.0 %collective-permute-done.37 = bf16[512,256]{1,0:T(8,128)(2,1)S(1)} collective-permute-done((bf16[512,256]{1,0:T(8,128)(2,1)S(1)}, bf16[512,256]{1,0:T(8,128)(2,1)S(1)}, u32[]{:S(2)}, u32[]{:S(2)}) %collective-permute-start.37) | collective-permute-done | bytes 262176 | tf_op jit(solution)/shard_map/ppermute | solution.py:218
  (162 shorter events, 65.3 us)
Async XLA Ops:
  1.1 16.2 %collective-permute-start = (bf16[512,256]{1,0:T(8,128)(2,1)S(1)}, bf16[512,256]{1,0:T(8,128)(2,1)S(1)}, u32[]{:S(2)}, u32[]{:S(2)}) collective-permute-start(bf16[512,256]{1,0:T(8,128)(2,1)S(1)} %get-tuple-element.108.refs_1_), channel_id=1, source_target_pairs={{0,2},{2,4},{4,6},{6,8},{8,10},{10,12},{12,14},{14,0},{1,3},{3,5},... | collective-permute-start | bytes 786440 | tf_op jit(solution)/shard_map/ppermute | solution.py:223
  3.1 14.2 %collective-permute-start.1 = (bf16[512,256]{1,0:T(8,128)(2,1)S(1)}, bf16[512,256]{1,0:T(8,128)(2,1)S(1)}, u32[]{:S(2)}, u32[]{:S(2)}) collective-permute-start(bf16[512,256]{1,0:T(8,128)(2,1)S(1)} %get-tuple-element.108.refs_1_), channel_id=1, source_target_pairs={{0,14},{2,0},{4,2},{6,4},{8,6},{10,8},{12,10},{14,12},{1,15},{3,1}... | collective-permute-start | bytes 786440 | tf_op jit(solution)/shard_map/ppermute | solution.py:226
  7.1 10.2 %collective-permute-start.2 = (bf16[512,256]{1,0:T(8,128)(2,1)S(1)}, bf16[512,256]{1,0:T(8,128)(2,1)S(1)}, u32[]{:S(2)}, u32[]{:S(2)}) collective-permute-start(bf16[512,256]{1,0:T(8,128)(2,1)S(1)} %get-tuple-element.107), channel_id=1, source_target_pairs={{0,1},{1,0},{2,3},{3,2},{4,5},{5,4},{6,7},{7,6},{8,9},{9,8},{10,11... | collective-permute-start | bytes 786440 | tf_op jit(solution)/shard_map/ppermute | solution.py:218
  17.3 48.5 %collective-permute-start.16 = (bf16[2,8,256,256]{3,2,1,0:T(8,128)(2,1)S(1)}, bf16[2,8,256,256]{3,2,1,0:T(8,128)(2,1)}, u32[]{:S(2)}, u32[]{:S(2)}) collective-permute-start(bf16[2,8,256,256]{3,2,1,0:T(8,128)(2,1)S(1)} %bitcast.47), channel_id=1, source_target_pairs={{0,1},{1,0},{2,3},{3,2},{4,5},{5,4},{6,7},{7,6},{8,9},{9,8},{10,11... | collective-permute-start | bytes 6291464 | tf_op jit(solution)/shard_map/ppermute | solution.py:218
  20.4 10.5 %collective-permute-start.4 = (bf16[512,256]{1,0:T(8,128)(2,1)S(1)}, bf16[512,256]{1,0:T(8,128)(2,1)S(1)}, u32[]{:S(2)}, u32[]{:S(2)}) collective-permute-start(bf16[512,256]{1,0:T(8,128)(2,1)S(1)} %collective-permute-done.refs_2_), channel_id=1, source_target_pairs={{0,2},{2,4},{4,6},{6,8},{8,10},{10,12},{12,14},{14,0},{1,3},{3,5},... | collective-permute-start | bytes 786440 | tf_op jit(solution)/shard_map/ppermute | solution.py:223
  20.4 10.5 %collective-permute-start.5 = (bf16[512,256]{1,0:T(8,128)(2,1)S(1)}, bf16[512,256]{1,0:T(8,128)(2,1)S(1)}, u32[]{:S(2)}, u32[]{:S(2)}) collective-permute-start(bf16[512,256]{1,0:T(8,128)(2,1)S(1)} %collective-permute-done.1.refs_6_), channel_id=1, source_target_pairs={{0,14},{2,0},{4,2},{6,4},{8,6},{10,8},{12,10},{14,12},{1,15},{3,1}... | collective-permute-start | bytes 786440 | tf_op jit(solution)/shard_map/ppermute | solution.py:226
  23.6 10.2 %collective-permute-start.6 = (bf16[512,256]{1,0:T(8,128)(2,1)S(1)}, bf16[512,256]{1,0:T(8,128)(2,1)S(1)}, u32[]{:S(2)}, u32[]{:S(2)}) collective-permute-start(bf16[512,256]{1,0:T(8,128)(2,1)S(1)} %collective-permute-done.2.refs_9_), channel_id=1, source_target_pairs={{0,2},{2,4},{4,6},{6,8},{8,10},{10,12},{12,14},{14,0},{1,3},{3,5},... | collective-permute-start | bytes 786440 | tf_op jit(solution)/shard_map/ppermute | solution.py:223
  23.6 10.2 %collective-permute-start.7 = (bf16[512,256]{1,0:T(8,128)(2,1)S(1)}, bf16[512,256]{1,0:T(8,128)(2,1)S(1)}, u32[]{:S(2)}, u32[]{:S(2)}) collective-permute-start(bf16[512,256]{1,0:T(8,128)(2,1)S(1)} %collective-permute-done.2.refs_9_), channel_id=1, source_target_pairs={{0,14},{2,0},{4,2},{6,4},{8,6},{10,8},{12,10},{14,12},{1,15},{3,1}... | collective-permute-start | bytes 786440 | tf_op jit(solution)/shard_map/ppermute | solution.py:226
  33.8 9.9 %collective-permute-start.10 = (bf16[512,256]{1,0:T(8,128)(2,1)S(1)}, bf16[512,256]{1,0:T(8,128)(2,1)S(1)}, u32[]{:S(2)}, u32[]{:S(2)}) collective-permute-start(bf16[512,256]{1,0:T(8,128)(2,1)S(1)} %collective-permute-done.6.refs_10_), channel_id=1, source_target_pairs={{0,2},{2,4},{4,6},{6,8},{8,10},{10,12},{12,14},{14,0},{1,3},{3,5},... | collective-permute-start | bytes 786440 | tf_op jit(solution)/shard_map/ppermute | solution.py:223
  33.9 9.8 %collective-permute-start.11 = (bf16[512,256]{1,0:T(8,128)(2,1)S(1)}, bf16[512,256]{1,0:T(8,128)(2,1)S(1)}, u32[]{:S(2)}, u32[]{:S(2)}) collective-permute-start(bf16[512,256]{1,0:T(8,128)(2,1)S(1)} %collective-permute-done.7.refs_13_), channel_id=1, source_target_pairs={{0,14},{2,0},{4,2},{6,4},{8,6},{10,8},{12,10},{14,12},{1,15},{3,1}... | collective-permute-start | bytes 786440 | tf_op jit(solution)/shard_map/ppermute | solution.py:226
  37.1 9.4 %collective-permute-start.9 = (bf16[512,256]{1,0:T(8,128)(2,1)S(1)}, bf16[512,256]{1,0:T(8,128)(2,1)S(1)}, u32[]{:S(2)}, u32[]{:S(2)}) collective-permute-start(bf16[512,256]{1,0:T(8,128)(2,1)S(1)} %collective-permute-done.5.refs_7_), channel_id=1, source_target_pairs={{0,14},{2,0},{4,2},{6,4},{8,6},{10,8},{12,10},{14,12},{1,15},{3,1}... | collective-permute-start | bytes 786440 | tf_op jit(solution)/shard_map/ppermute | solution.py:226
  47.9 10.4 %collective-permute-start.13 = (bf16[512,256]{1,0:T(8,128)(2,1)S(1)}, bf16[512,256]{1,0:T(8,128)(2,1)S(1)}, u32[]{:S(2)}, u32[]{:S(2)}) collective-permute-start(bf16[512,256]{1,0:T(8,128)(2,1)S(1)} %collective-permute-done.10.refs_11_), channel_id=1, source_target_pairs={{0,2},{2,4},{4,6},{6,8},{8,10},{10,12},{12,14},{14,0},{1,3},{3,5},... | collective-permute-start | bytes 786440 | tf_op jit(solution)/shard_map/ppermute | solution.py:223
  65.8 27.8 %collective-permute-start.17 = (bf16[1,8,256,256]{3,2,1,0:T(8,128)(2,1)}, bf16[1,8,256,256]{3,2,1,0:T(8,128)(2,1)}, u32[]{:S(2)}, u32[]{:S(2)}) collective-permute-start(bf16[1,8,256,256]{3,2,1,0:T(8,128)(2,1)} %bitcast.14), channel_id=1, source_target_pairs={{0,1},{1,0},{2,3},{3,2},{4,5},{5,4},{6,7},{7,6},{8,9},{9,8},{10,11... | collective-permute-start | bytes 3145736 | tf_op jit(solution)/shard_map/ppermute | solution.py:218
  97.0 27.1 %collective-permute-start.23 = (bf16[256,2048]{1,0:T(8,128)(2,1)S(1)}, bf16[256,2048]{1,0:T(8,128)(2,1)S(1)}, u32[]{:S(2)}, u32[]{:S(2)}) collective-permute-start(bf16[256,2048]{1,0:T(8,128)(2,1)S(1)} %constant_dynamic-slice_fusion.1), channel_id=1, source_target_pairs={{0,1},{1,0},{2,3},{3,2},{4,5},{5,4},{6,7},{7,6},{8,9},{9,8},{10,11... | collective-permute-start | bytes 3145736 | tf_op jit(solution)/shard_map/ppermute | solution.py:218
  102.0 11.2 %collective-permute-start.24 = (f32[16,512]{1,0:T(8,128)}, f32[16,512]{1,0:T(8,128)S(1)}, u32[]{:S(2)}, u32[]{:S(2)}) collective-permute-start(f32[16,512]{1,0:T(8,128)} %get-tuple-element.83), channel_id=1, source_target_pairs={{0,64},{64,128},{128,192},{192,0},{1,65},{65,129},{129,193},{193,1... | collective-permute-start | bytes 98312 | tf_op jit(solution)/shard_map/ppermute | solution.py:319
  103.6 9.7 %collective-permute-start.25 = (f32[16,512]{1,0:T(8,128)}, f32[16,512]{1,0:T(8,128)S(1)}, u32[]{:S(2)}, u32[]{:S(2)}) collective-permute-start(f32[16,512]{1,0:T(8,128)} %get-tuple-element.84), channel_id=1, source_target_pairs={{0,192},{64,0},{128,64},{192,128},{1,193},{65,1},{129,65},{193,129... | collective-permute-start | bytes 98312 | tf_op jit(solution)/shard_map/ppermute | solution.py:319
  139.1 9.8 %collective-permute-start.29 = (bf16[256,512]{1,0:T(8,128)(2,1)}, bf16[256,512]{1,0:T(8,128)(2,1)S(1)}, u32[]{:S(2)}, u32[]{:S(2)}) collective-permute-start(bf16[256,512]{1,0:T(8,128)(2,1)} %get-tuple-element.96), channel_id=1, source_target_pairs={{0,2},{2,4},{4,6},{6,8},{8,10},{10,12},{12,14},{14,0},{1,3},{3,5},... | collective-permute-start | bytes 786440 | tf_op jit(solution)/shard_map/ppermute | solution.py:223
  140.2 9.9 %collective-permute-start.33 = (bf16[256,512]{1,0:T(8,128)(2,1)}, bf16[256,512]{1,0:T(8,128)(2,1)S(1)}, u32[]{:S(2)}, u32[]{:S(2)}) collective-permute-start(bf16[256,512]{1,0:T(8,128)(2,1)} %get-tuple-element.101), channel_id=1, source_target_pairs={{0,14},{2,0},{4,2},{6,4},{8,6},{10,8},{12,10},{14,12},{1,15},{3,1}... | collective-permute-start | bytes 786440 | tf_op jit(solution)/shard_map/ppermute | solution.py:226
  150.0 14.4 %collective-permute-start.30 = (bf16[512,512]{1,0:T(8,128)(2,1)S(1)}, bf16[512,512]{1,0:T(8,128)(2,1)S(1)}, u32[]{:S(2)}, u32[]{:S(2)}) collective-permute-start(bf16[512,512]{1,0:T(8,128)(2,1)S(1)} %pad_maximum_fusion), channel_id=1, source_target_pairs={{0,2},{2,4},{4,6},{6,8},{8,10},{10,12},{12,14},{14,0},{1,3},{3,5},... | collective-permute-start | bytes 1572872 | tf_op jit(solution)/shard_map/ppermute | solution.py:223
  150.3 14.4 %collective-permute-start.34 = (bf16[512,512]{1,0:T(8,128)(2,1)S(1)}, bf16[512,512]{1,0:T(8,128)(2,1)S(1)}, u32[]{:S(2)}, u32[]{:S(2)}) collective-permute-start(bf16[512,512]{1,0:T(8,128)(2,1)S(1)} %pad_maximum_fusion.1), channel_id=1, source_target_pairs={{0,14},{2,0},{4,2},{6,4},{8,6},{10,8},{12,10},{14,12},{1,15},{3,1}... | collective-permute-start | bytes 1572872 | tf_op jit(solution)/shard_map/ppermute | solution.py:226
  164.6 13.5 %collective-permute-start.31 = (bf16[512,512]{1,0:T(8,128)(2,1)S(1)}, bf16[512,512]{1,0:T(8,128)(2,1)S(1)}, u32[]{:S(2)}, u32[]{:S(2)}) collective-permute-start(bf16[512,512]{1,0:T(8,128)(2,1)S(1)} %add_convert_fusion.4), channel_id=1, source_target_pairs={{0,2},{2,4},{4,6},{6,8},{8,10},{10,12},{12,14},{14,0},{1,3},{3,5},... | collective-permute-start | bytes 1572872 | tf_op jit(solution)/shard_map/ppermute | solution.py:223
  164.9 13.5 %collective-permute-start.35 = (bf16[512,512]{1,0:T(8,128)(2,1)S(1)}, bf16[512,512]{1,0:T(8,128)(2,1)S(1)}, u32[]{:S(2)}, u32[]{:S(2)}) collective-permute-start(bf16[512,512]{1,0:T(8,128)(2,1)S(1)} %add_convert_fusion.2), channel_id=1, source_target_pairs={{0,14},{2,0},{4,2},{6,4},{8,6},{10,8},{12,10},{14,12},{1,15},{3,1}... | collective-permute-start | bytes 1572872 | tf_op jit(solution)/shard_map/ppermute | solution.py:226
  178.2 12.6 %collective-permute-start.32 = (bf16[512,512]{1,0:T(8,128)(2,1)S(1)}, bf16[512,512]{1,0:T(8,128)(2,1)S(1)}, u32[]{:S(2)}, u32[]{:S(2)}) collective-permute-start(bf16[512,512]{1,0:T(8,128)(2,1)S(1)} %add_convert_fusion.3), channel_id=1, source_target_pairs={{0,2},{2,4},{4,6},{6,8},{8,10},{10,12},{12,14},{14,0},{1,3},{3,5},... | collective-permute-start | bytes 1572872 | tf_op jit(solution)/shard_map/ppermute | solution.py:223
  178.5 12.3 %collective-permute-start.36 = (bf16[512,512]{1,0:T(8,128)(2,1)S(1)}, bf16[512,512]{1,0:T(8,128)(2,1)S(1)}, u32[]{:S(2)}, u32[]{:S(2)}) collective-permute-start(bf16[512,512]{1,0:T(8,128)(2,1)S(1)} %add_convert_fusion.1), channel_id=1, source_target_pairs={{0,14},{2,0},{4,2},{6,4},{8,6},{10,8},{12,10},{14,12},{1,15},{3,1}... | collective-permute-start | bytes 1572872 | tf_op jit(solution)/shard_map/ppermute | solution.py:226
  (50 other events, 803.9 us)
where the time goes:
time: 201 us; the launch traced here: 200 us
  waiting for transfers between devices  85.3 us (42%)
  starting transfers between devices  59.7 us (30%)
  Pallas kernels  32.9 us (16%)
  local copies, waits for them, and re-layouts  15.3 us (8%)
  other arithmetic  6.23 us (3%)
    ppermute x11, waiting for transfers between devices, ahead_z(): return lax.ppermute(x, 'z', around(n_z, 1))  54.6 us
    ppermute x11, starting transfers between devices, back_z(): return lax.ppermute(x, 'z', around(n_z, -1))  32.9 us
    ppermute x9, waiting for transfers between devices, swap(): return lax.ppermute(piece, axis, SWAP)  23.7 us
    pallas_call x1, Pallas kernels, per_device(): pl.pallas_call(lambda *refs: project_all(*refs, n_chunks=len(chunks)), in...  13.9 us
    ppermute x9, starting transfers between devices, swap(): return lax.ppermute(piece, axis, SWAP)  13 us
    pallas_call x1, Pallas kernels, per_device(): pl.pallas_call(lambda *refs: convolve_and_project(*refs, n_given=len(give...  11.3 us
    pallas_call x1, Pallas kernels, per_device(): pl.pallas_call(lambda *refs: project_query(*refs, n_chunks=len(chunks)),...  5.88 us
    ppermute x11, starting transfers between devices, ahead_z(): return lax.ppermute(x, 'z', around(n_z, 1))  5.63 us
  transfers between devices with their start and end apart: 38, of which 21 were waited for; matrix products, arithmetic and copies ran while one was open for 7% of the time, Pallas kernels for 11%

commit v1 on v0

--- a/solution.py
+++ b/solution.py
@@ -124,21 +124,12 @@
         out[...] = total
 
 
-def convolve_and_project(where, *refs, n_given, n_parts, n_outs):
+def convolve(*refs, n_given):
     given = refs[:n_given]
-    ends, mixed, query_own, query_peer, rates, gains, skip, out_own = refs[n_given : n_given + 8]
-    parts = refs[n_given + 8 : n_given + 8 + n_parts]
-    outs = refs[n_given + 8 + n_parts : n_given + 8 + n_parts + n_outs]
-    mixed_rows, conv_rows, gated, own_cols, peer_cols, stage, sems = refs[n_given + 8 + n_parts + n_outs :]
+    ends, mixed, query_own, query_peer, rates, gains, skip, gated, mixed_rows, conv_rows = refs[n_given:]
     tokens, width = mixed.shape
     half = width // 2
     steps = tokens // SEGS
-    cols = outs[0].shape[1]
-    deep = parts[0].shape[1]
-    pltpu.make_async_copy(out_own, own_cols, sems.at[0]).start()
-    for i, part in enumerate(parts):
-        target = peer_cols.at[:, pl.ds(pl.multiple_of(where[i] * deep, deep), deep)]
-        pltpu.make_async_copy(part, target, sems.at[1]).start()
     for g in range(width // 128):
         mixed_rows[g] = mixed[:, g * 128 : (g + 1) * 128].astype(F32)
     incoming = given[0][...]
@@ -176,27 +167,45 @@
         inner = conv_rows[g] + skip[:, lanes] * mixed_rows[g]
         query = (query_own, query_peer)[g * 128 // half]
         gated[:, lanes] = (query[:, g * 128 % half : g * 128 % half + 128].astype(F32) * inner).astype(BF16)
+
+
+def project_out(where, gated, out_own, *refs, first, n_parts, n_outs):
+    parts, outs = refs[:n_parts], refs[n_parts : n_parts + n_outs]
+    own_cols, peer_cols, stage, sems = refs[n_parts + n_outs :]
+    tokens, half = gated.shape[0], gated.shape[1] // 2
+    blocks, cols = stage.shape[0], stage.shape[2]
+    deep = parts[0].shape[1]
+
+    def place(i):
+        return pl.ds(pl.multiple_of(where[n_parts + first + i] * cols, cols), cols)
+
+    for i in range(blocks):
+        pltpu.make_async_copy(out_own.at[:, place(i)], own_cols.at[i], sems.at[0]).start()
+    for i, part in enumerate(parts):
+        target = peer_cols.at[:, pl.ds(pl.multiple_of(where[i] * deep, deep), deep)]
+        pltpu.make_async_copy(part, target, sems.at[1]).start()
     pltpu.make_async_copy(own_cols, own_cols, sems.at[0]).wait()
     pltpu.make_async_copy(peer_cols, peer_cols, sems.at[1]).wait()
 
     def block(i, _):
-        k = where[len(parts) + i]
-        place = pl.multiple_of(k * cols, cols)
-        own = jnp.dot(gated[:, :half], own_cols[:, pl.ds(place, cols)], preferred_element_type=F32)
-        peer = jnp.dot(gated[:, half:], peer_cols[:, pl.ds(place, cols)], preferred_element_type=F32)
+        own = jnp.dot(gated[:, :half], own_cols[i], preferred_element_type=F32)
+        peer = jnp.dot(gated[:, half:], peer_cols[:, place(i)], preferred_element_type=F32)
         stage[i] = (own + peer).astype(BF16)
         return 0
 
     copies = []
-    for first in (0, 4):
-        lax.fori_loop(first, first + 4, block, 0)
-        for i in range(first, first + 4):
-            for out, rows in ((outs[0], pl.ds(0, tokens // 2)), (outs[1], pl.ds(tokens // 2, tokens // 2))):
-                if i > 0:
-                    out, rows = outs[i + 1], pl.ds(0, tokens)
-                if i == 0 or len(copies) < i + 2:
-                    copies.append(pltpu.make_async_copy(stage.at[i, rows, :], out, sems.at[2 + len(copies)]))
-                    copies[-1].start()
+    if blocks == 1:
+        block(0, 0)
+        for i, out in enumerate(outs):
+            rows = pl.ds(i * (tokens // 2), tokens // 2)
+            copies.append(pltpu.make_async_copy(stage.at[0, rows, :], out, sems.at[2 + i]))
+            copies[-1].start()
+    else:
+        for start, stop in ((0, 4), (4, blocks)):
+            lax.fori_loop(start, stop, block, 0)
+            for i in range(start, stop):
+                copies.append(pltpu.make_async_copy(stage.at[i], outs[i], sems.at[2 + i]))
+                copies[-1].start()
     for copy in copies:
         copy.wait()
 
@@ -318,47 +327,41 @@
     )(lags, *pieces, rates)
     given = [given[0]] + [lax.ppermute(g, "y", around(n_y, o)) for g, o in zip(given[1:], ahead[1:])]
 
-    out_part, given, query_peer = together((out_part, given, query_peer))
+    gated = pl.pallas_call(
+        lambda *refs: convolve(*refs, n_given=len(given)),
+        in_specs=[VMEM] * (len(given) + 7),
+        out_specs=VMEM,
+        out_shape=jax.ShapeDtypeStruct((tokens, 2 * width), BF16),
+        scratch_shapes=[pltpu.VMEM((2 * width // 128, tokens, 128), F32)] * 2,
+        compiler_params=params,
+    )(*given, ends, mixed, query_own, query_peer, rates, gains, skip)
+    out_part, gated = together((out_part, gated))
     out_parts = [out_part, swap(out_part, "core")]
-    n_outs = len(reach) + 1
-    full = jax.ShapeDtypeStruct((tokens, out_cols), BF16)
-    half_rows = jax.ShapeDtypeStruct((tokens // 2, out_cols), BF16)
-    outs = pl.pallas_call(
-        lambda *refs: convolve_and_project(*refs, n_given=len(given), n_parts=len(out_parts), n_outs=n_outs),
-        in_specs=[SMEM] + [VMEM] * (len(given) + 7) + [HBM] * (1 + len(out_parts)),
-        out_specs=[HBM] * n_outs,
-        out_shape=[half_rows] * 2 + [full] * (n_outs - 2),
-        scratch_shapes=[
-            pltpu.VMEM((2 * width // 128, tokens, 128), F32),
-            pltpu.VMEM((2 * width // 128, tokens, 128), F32),
-            pltpu.VMEM((tokens, 2 * width), BF16),
-            pltpu.VMEM(out_weight.shape, BF16),
-            pltpu.VMEM(out_weight.shape, BF16),
-            pltpu.VMEM((len(reach), tokens, out_cols), BF16),
-            pltpu.SemaphoreType.DMA((2 + n_outs,)),
-        ],
-        compiler_params=params,
-    )(
-        where_out,
-        *given,
-        ends,
-        mixed,
-        query_own,
-        query_peer,
-        rates,
-        gains,
-        skip,
-        out_weight,
-        *out_parts,
-    )
-    share = dict(zip(reach[1:], outs[2:]))
-    low, high = slice(0, tokens // 2), slice(tokens // 2, tokens)
+
+    def project_cols(first, blocks, out_shape):
+        return pl.pallas_call(
+            lambda *refs: project_out(*refs, first=first, n_parts=len(out_parts), n_outs=len(out_shape)),
+            in_specs=[SMEM, VMEM] + [HBM] * (1 + len(out_parts)),
+            out_specs=[HBM] * len(out_shape),
+            out_shape=out_shape,
+            scratch_shapes=[
+                pltpu.VMEM((blocks, width, out_cols), BF16),
+                pltpu.VMEM(out_weight.shape, BF16),
+                pltpu.VMEM((blocks, tokens, out_cols), BF16),
+                pltpu.SemaphoreType.DMA((2 + len(out_shape),)),
+            ],
+            compiler_params=params,
+        )(where_out, gated, out_weight, *out_parts)
+
+    farthest = project_cols(0, 1, [jax.ShapeDtypeStruct((tokens // 2, out_cols), BF16)] * 2)
+    nearer = project_cols(1, len(reach) - 1, [jax.ShapeDtypeStruct((tokens, out_cols), BF16)] * (len(reach) - 1))
+    share = dict(zip(reach[1:], nearer))
 
     def add(a, b):
         return (a.astype(F32) + b.astype(F32)).astype(BF16)
 
-    forward = jnp.concatenate([add(ahead_z(outs[0]), share[3][low]), share[3][high]], 0)
-    backward = jnp.concatenate([share[-3][low], add(back_z(outs[1]), share[-3][high])], 0)
+    forward = add(jnp.pad(ahead_z(farthest[0]).astype(F32), ((0, tokens // 2), (0, 0))), share[3])
+    backward = add(jnp.pad(back_z(farthest[1]).astype(F32), ((tokens // 2, 0), (0, 0))), share[-3])
     for hop in (2, 1):
         forward = add(ahead_z(forward), share[hop])
         backward = add(back_z(backward), share[-hop])

time: 201 us -> 195 us (0.970)
  waiting for transfers between devices: 85.3 us -> 72.1 us
  Pallas kernels: 32.9 us -> 40.2 us
    ppermute x9, waiting for transfers between devices: 23.7 us -> 16.1 us  [swap(): return lax.ppermute(piece, axis, SWAP)]
    pallas_call x1 -> x3, Pallas kernels: 11.3 us -> 18.7 us  [the longest x2 11.5 us: project_cols(): pl.pallas_call(lambda *refs: project_out(*refs, first=first, n_parts=len(...]
    ppermute x11, waiting for transfers between devices: 54.6 us -> 48.7 us  [ahead_z(): return lax.ppermute(x, 'z', around(n_z, 1))]
    slice x2 -> x0, local copies, waits for them, and re-layouts: 2.02 us -> none  [the longest x1 1.03 us: per_device(): share[-3][low]]
    unnamed x72 -> x70, local copies, waits for them, and re-layouts: 4.74 us -> 5.34 us
  transfers between devices with their start and end apart: 38 -> 38, of which waited for: 21 -> 21; matrix products, arithmetic and copies ran while one was open for 7% -> 7% of each run, Pallas kernels for 11% -> 19%
where the time goes in v1:
time: 195 us
  waiting for transfers between devices  72.1 us (37%)
  starting transfers between devices  60.7 us (31%)
  Pallas kernels  40.2 us (21%)
  local copies, waits for them, and re-layouts  13.7 us (7%)
  other arithmetic  7.44 us (4%)
    ppermute x11, waiting for transfers between devices, ahead_z(): return lax.ppermute(x, 'z', around(n_z, 1))  48.7 us
    ppermute x11, starting transfers between devices, back_z(): return lax.ppermute(x, 'z', around(n_z, -1))  33.8 us
    ppermute x9, waiting for transfers between devices, swap(): return lax.ppermute(piece, axis, SWAP)  16.1 us
    pallas_call x1, Pallas kernels, per_device(): pl.pallas_call(lambda *refs: project_all(*refs, n_chunks=len(chunks)), in...  13.9 us
    ppermute x9, starting transfers between devices, swap(): return lax.ppermute(piece, axis, SWAP)  13 us
    pallas_call x2, Pallas kernels, project_cols(): pl.pallas_call(lambda *refs: project_out(*refs, first=first, n_parts=len(...  11.5 us
    pallas_call x1, Pallas kernels, per_device(): pl.pallas_call(lambda *refs: convolve(*refs, n_given=len(given)), in_spec...  7.2 us
    pallas_call x1, Pallas kernels, per_device(): pl.pallas_call(lambda *refs: project_query(*refs, n_chunks=len(chunks)),...  5.88 us
  transfers between devices with their start and end apart: 38, of which 21 were waited for; matrix products, arithmetic and copies ran while one was open for 7% of the time, Pallas kernels for 19%

profile of v1, /device:TPU:8, one launch (start us, length us, event | category | flops | bytes accessed | tf_op | source)
XLA Modules:
  0.0 194.6 jit_solution(8488285125067013761)
XLA Ops:
  3.1 4.0 %collective-permute-start.1 = (bf16[512,256]{1,0:T(8,128)(2,1)S(1)}, bf16[512,256]{1,0:T(8,128)(2,1)S(1)}, u32[]{:S(2)}, u32[]{:S(2)}) collective-permute-start(bf16[512,256]{1,0:T(8,128)(2,1)S(1)} %get-tuple-element.100.refs_1_), channel_id=1, source_target_pairs={{0,14},{2,0},{4,2},{6,4},{8,6},{10,8},{12,10},{14,12},{1,15},{3,1}... | collective-permute-start | bytes 786440 | tf_op jit(solution)/shard_map/ppermute | solution.py:235
  7.1 3.0 %collective-permute-start.2 = (bf16[512,256]{1,0:T(8,128)(2,1)S(1)}, bf16[512,256]{1,0:T(8,128)(2,1)S(1)}, u32[]{:S(2)}, u32[]{:S(2)}) collective-permute-start(bf16[512,256]{1,0:T(8,128)(2,1)S(1)} %get-tuple-element.99), channel_id=1, source_target_pairs={{0,1},{1,0},{2,3},{3,2},{4,5},{5,4},{6,7},{7,6},{8,9},{9,8},{10,11... | collective-permute-start | bytes 786440 | tf_op jit(solution)/shard_map/ppermute | solution.py:227
  13.2 4.1 %collective-permute-done.3 = f32[33,256]{1,0:T(8,128)S(1)} collective-permute-done((f32[33,256]{1,0:T(8,128)S(1)}, f32[33,256]{1,0:T(8,128)S(1)}, u32[]{:S(2)}, u32[]{:S(2)}) %collective-permute-start.3) | collective-permute-done | bytes 33824 | tf_op jit(solution)/shard_map/ppermute | solution.py:227
  17.3 3.1 %collective-permute-start.16 = (bf16[2,8,256,256]{3,2,1,0:T(8,128)(2,1)S(1)}, bf16[2,8,256,256]{3,2,1,0:T(8,128)(2,1)}, u32[]{:S(2)}, u32[]{:S(2)}) collective-permute-start(bf16[2,8,256,256]{3,2,1,0:T(8,128)(2,1)S(1)} %bitcast.47), channel_id=1, source_target_pairs={{0,1},{1,0},{2,3},{3,2},{4,5},{5,4},{6,7},{7,6},{8,9},{9,8},{10,11... | collective-permute-start | bytes 6291464 | tf_op jit(solution)/shard_map/ppermute | solution.py:227
  20.4 3.2 %collective-permute-start.5 = (bf16[512,256]{1,0:T(8,128)(2,1)S(1)}, bf16[512,256]{1,0:T(8,128)(2,1)S(1)}, u32[]{:S(2)}, u32[]{:S(2)}) collective-permute-start(bf16[512,256]{1,0:T(8,128)(2,1)S(1)} %collective-permute-done.1.refs_6_), channel_id=1, source_target_pairs={{0,14},{2,0},{4,2},{6,4},{8,6},{10,8},{12,10},{14,12},{1,15},{3,1}... | collective-permute-start | bytes 786440 | tf_op jit(solution)/shard_map/ppermute | solution.py:235
  23.6 3.2 %collective-permute-start.7 = (bf16[512,256]{1,0:T(8,128)(2,1)S(1)}, bf16[512,256]{1,0:T(8,128)(2,1)S(1)}, u32[]{:S(2)}, u32[]{:S(2)}) collective-permute-start(bf16[512,256]{1,0:T(8,128)(2,1)S(1)} %collective-permute-done.2.refs_9_), channel_id=1, source_target_pairs={{0,14},{2,0},{4,2},{6,4},{8,6},{10,8},{12,10},{14,12},{1,15},{3,1}... | collective-permute-start | bytes 786440 | tf_op jit(solution)/shard_map/ppermute | solution.py:235
  26.9 4.0 %collective-permute-done.4.refs_3_ = bf16[512,256]{1,0:T(8,128)(2,1)S(1)} collective-permute-done((bf16[512,256]{1,0:T(8,128)(2,1)S(1)}, bf16[512,256]{1,0:T(8,128)(2,1)S(1)}, u32[]{:S(2)}, u32[]{:S(2)}) %collective-permute-start.4) | collective-permute-done | bytes 262176 | tf_op jit(solution)/shard_map/ppermute | solution.py:232
  33.9 3.2 %collective-permute-start.11 = (bf16[512,256]{1,0:T(8,128)(2,1)S(1)}, bf16[512,256]{1,0:T(8,128)(2,1)S(1)}, u32[]{:S(2)}, u32[]{:S(2)}) collective-permute-start(bf16[512,256]{1,0:T(8,128)(2,1)S(1)} %collective-permute-done.7.refs_13_), channel_id=1, source_target_pairs={{0,14},{2,0},{4,2},{6,4},{8,6},{10,8},{12,10},{14,12},{1,15},{3,1}... | collective-permute-start | bytes 786440 | tf_op jit(solution)/shard_map/ppermute | solution.py:235
  37.1 3.2 %collective-permute-start.9 = (bf16[512,256]{1,0:T(8,128)(2,1)S(1)}, bf16[512,256]{1,0:T(8,128)(2,1)S(1)}, u32[]{:S(2)}, u32[]{:S(2)}) collective-permute-start(bf16[512,256]{1,0:T(8,128)(2,1)S(1)} %collective-permute-done.5.refs_7_), channel_id=1, source_target_pairs={{0,14},{2,0},{4,2},{6,4},{8,6},{10,8},{12,10},{14,12},{1,15},{3,1}... | collective-permute-start | bytes 786440 | tf_op jit(solution)/shard_map/ppermute | solution.py:235
  40.4 3.3 %collective-permute-done.10.refs_11_ = bf16[512,256]{1,0:T(8,128)(2,1)S(1)} collective-permute-done((bf16[512,256]{1,0:T(8,128)(2,1)S(1)}, bf16[512,256]{1,0:T(8,128)(2,1)S(1)}, u32[]{:S(2)}, u32[]{:S(2)}) %collective-permute-start.10) | collective-permute-done | bytes 262176 | tf_op jit(solution)/shard_map/ppermute | solution.py:232
  51.2 4.4 %collective-permute-done.12.refs_5_ = bf16[512,256]{1,0:T(8,128)(2,1)S(1)} collective-permute-done((bf16[512,256]{1,0:T(8,128)(2,1)S(1)}, bf16[512,256]{1,0:T(8,128)(2,1)S(1)}, u32[]{:S(2)}, u32[]{:S(2)}) %collective-permute-start.12) | collective-permute-done | bytes 262176 | tf_op jit(solution)/shard_map/ppermute | solution.py:232
  71.5 13.9 %shard_map.73 = (bf16[512,512]{1,0:T(8,128)(2,1)}, f32[16,8,512]{2,1,0:T(8,128)}, f32[16,512]{1,0:T(8,128)}, bf16[512,256]{1,0:T(8,128)(2,1)}) custom-call(s32[18]{0:T(128)} %stack.170.refs_0_, bf16[512,256]{1,0:T(8,128)(2,1)} %copy-done.3, bf16[512,256]{1,0:T(8,128)(2,1)} %copy-done.5, bf16[512,256]{1,0:T(8,128)(2,1)} %copy-done.8, ...), custom_call_target="tpu_custom_call" | custom-call | tf_op jit(solution)/shard_map/pallas_call | solution.py:263
  107.9 5.9 %shard_map.75.refs_7_ = bf16[512,256]{1,0:T(8,128)(2,1)} custom-call(s32[18]{0:T(128)} %stack.170.refs_0_, bf16[512,256]{1,0:T(8,128)(2,1)} %copy-done.3, bf16[512,256]{1,0:T(8,128)(2,1)} %copy-done.5, bf16[512,256]{1,0:T(8,128)(2,1)} %copy-done.8, bf16[512,256]{1,0:T(8,128)(2,1)} %copy-done.14, bf16[512,256]{1,0:T(8,128)(2,1)} %copy-done.16, ...), custom_call_target="tpu_custom_call" | custom-call | tf_op jit(solution)/shard_map/pallas_call | solution.py:295
  114.5 7.2 %shard_map.76.refs_1_ = bf16[512,512]{1,0:T(8,128)(2,1)} custom-call(f32[16,512]{1,0:T(8,128)} %get-tuple-element.78.refs_0_, f32[16,512]{1,0:T(8,128)} %copy-done.30, f32[16,512]{1,0:T(8,128)} %copy-done.31, f32[16,512]{1,0:T(8,128)} %copy-done.32, f32[16,8,512]{2,1,0:T(8,128)} %get-tuple-element.82.refs_4_, bf16[512,512]{1,0:T(8,128)(2,1)} %get-tuple-element.83.refs_5_, ...), custom_call_target="tpu_custom_call" | custom-call | tf_op jit(solution)/shard_map/pallas_call | solution.py:330
  127.8 4.0 %shard_map.77 = (bf16[256,512]{1,0:T(8,128)(2,1)}, bf16[256,512]{1,0:T(8,128)(2,1)}) custom-call(s32[10]{0:T(128)} %stack.151.refs_0_, bf16[512,512]{1,0:T(8,128)(2,1)} %shard_map.76.refs_1_, bf16[256,4096]{1,0:T(8,128)(2,1)} %refs_2_.3, bf16[256,2048]{1,0:T(8,128)(2,1)} %copy-done.1, bf16[256,2048]{1,0:T(8,128)(2,1)} %copy-done.2), custom_call_target="tpu_custom_call" | custom-call | tf_op jit(solution)/shard_map/pallas_call | solution.py:342
  131.9 3.2 %collective-permute-start.33 = (bf16[256,512]{1,0:T(8,128)(2,1)}, bf16[256,512]{1,0:T(8,128)(2,1)S(1)}, u32[]{:S(2)}, u32[]{:S(2)}) collective-permute-start(bf16[256,512]{1,0:T(8,128)(2,1)} %get-tuple-element.92), channel_id=1, source_target_pairs={{0,14},{2,0},{4,2},{6,4},{8,6},{10,8},{12,10},{14,12},{1,15},{3,1}... | collective-permute-start | bytes 786440 | tf_op jit(solution)/shard_map/ppermute | solution.py:235
  135.0 7.5 %shard_map.78 = (bf16[512,512]{1,0:T(8,128)(2,1)}, bf16[512,512]{1,0:T(8,128)(2,1)}, bf16[512,512]{1,0:T(8,128)(2,1)}, bf16[512,512]{1,0:T(8,128)(2,1)}, bf16[51...) custom-call(s32[10]{0:T(128)} %stack.151.refs_0_, bf16[512,512]{1,0:T(8,128)(2,1)} %shard_map.76.refs_1_, ...), custom_call_target="tpu_custom_call" | custom-call | tf_op jit(solution)/shard_map/pallas_call | solution.py:342
  145.1 3.3 %collective-permute-start.34 = (bf16[512,512]{1,0:T(8,128)(2,1)S(1)}, bf16[512,512]{1,0:T(8,128)(2,1)S(1)}, u32[]{:S(2)}, u32[]{:S(2)}) collective-permute-start(bf16[512,512]{1,0:T(8,128)(2,1)S(1)} %add_convert_fusion.3), channel_id=1, source_target_pairs={{0,14},{2,0},{4,2},{6,4},{8,6},{10,8},{12,10},{14,12},{1,15},{3,1}... | collective-permute-start | bytes 1572872 | tf_op jit(solution)/shard_map/ppermute | solution.py:235
  148.4 10.1 %collective-permute-done.30 = bf16[512,512]{1,0:T(8,128)(2,1)S(1)} collective-permute-done((bf16[512,512]{1,0:T(8,128)(2,1)S(1)}, bf16[512,512]{1,0:T(8,128)(2,1)S(1)}, u32[]{:S(2)}, u32[]{:S(2)}) %collective-permute-start.30) | collective-permute-done | bytes 524320 | tf_op jit(solution)/shard_map/ppermute | solution.py:232
  159.2 3.8 %collective-permute-start.35 = (bf16[512,512]{1,0:T(8,128)(2,1)S(1)}, bf16[512,512]{1,0:T(8,128)(2,1)S(1)}, u32[]{:S(2)}, u32[]{:S(2)}) collective-permute-start(bf16[512,512]{1,0:T(8,128)(2,1)S(1)} %add_convert_fusion.2), channel_id=1, source_target_pairs={{0,14},{2,0},{4,2},{6,4},{8,6},{10,8},{12,10},{14,12},{1,15},{3,1}... | collective-permute-start | bytes 1572872 | tf_op jit(solution)/shard_map/ppermute | solution.py:235
  162.9 9.5 %collective-permute-done.31 = bf16[512,512]{1,0:T(8,128)(2,1)S(1)} collective-permute-done((bf16[512,512]{1,0:T(8,128)(2,1)S(1)}, bf16[512,512]{1,0:T(8,128)(2,1)S(1)}, u32[]{:S(2)}, u32[]{:S(2)}) %collective-permute-start.31) | collective-permute-done | bytes 524320 | tf_op jit(solution)/shard_map/ppermute | solution.py:232
  172.8 3.7 %collective-permute-start.36 = (bf16[512,512]{1,0:T(8,128)(2,1)S(1)}, bf16[512,512]{1,0:T(8,128)(2,1)S(1)}, u32[]{:S(2)}, u32[]{:S(2)}) collective-permute-start(bf16[512,512]{1,0:T(8,128)(2,1)S(1)} %add_convert_fusion.1), channel_id=1, source_target_pairs={{0,14},{2,0},{4,2},{6,4},{8,6},{10,8},{12,10},{14,12},{1,15},{3,1}... | collective-permute-start | bytes 1572872 | tf_op jit(solution)/shard_map/ppermute | solution.py:235
  176.6 8.9 %collective-permute-done.32 = bf16[512,512]{1,0:T(8,128)(2,1)S(1)} collective-permute-done((bf16[512,512]{1,0:T(8,128)(2,1)S(1)}, bf16[512,512]{1,0:T(8,128)(2,1)S(1)}, u32[]{:S(2)}, u32[]{:S(2)}) %collective-permute-start.32) | collective-permute-done | bytes 524320 | tf_op jit(solution)/shard_map/ppermute | solution.py:232
  187.7 6.0 %collective-permute-done.37 = bf16[512,256]{1,0:T(8,128)(2,1)S(1)} collective-permute-done((bf16[512,256]{1,0:T(8,128)(2,1)S(1)}, bf16[512,256]{1,0:T(8,128)(2,1)S(1)}, u32[]{:S(2)}, u32[]{:S(2)}) %collective-permute-start.37) | collective-permute-done | bytes 262176 | tf_op jit(solution)/shard_map/ppermute | solution.py:227
  (158 shorter events, 68.4 us)
Async XLA Ops:
  1.1 16.2 %collective-permute-start = (bf16[512,256]{1,0:T(8,128)(2,1)S(1)}, bf16[512,256]{1,0:T(8,128)(2,1)S(1)}, u32[]{:S(2)}, u32[]{:S(2)}) collective-permute-start(bf16[512,256]{1,0:T(8,128)(2,1)S(1)} %get-tuple-element.100.refs_1_), channel_id=1, source_target_pairs={{0,2},{2,4},{4,6},{6,8},{8,10},{10,12},{12,14},{14,0},{1,3},{3,5},... | collective-permute-start | bytes 786440 | tf_op jit(solution)/shard_map/ppermute | solution.py:232
  3.1 14.2 %collective-permute-start.1 = (bf16[512,256]{1,0:T(8,128)(2,1)S(1)}, bf16[512,256]{1,0:T(8,128)(2,1)S(1)}, u32[]{:S(2)}, u32[]{:S(2)}) collective-permute-start(bf16[512,256]{1,0:T(8,128)(2,1)S(1)} %get-tuple-element.100.refs_1_), channel_id=1, source_target_pairs={{0,14},{2,0},{4,2},{6,4},{8,6},{10,8},{12,10},{14,12},{1,15},{3,1}... | collective-permute-start | bytes 786440 | tf_op jit(solution)/shard_map/ppermute | solution.py:235
  7.1 10.2 %collective-permute-start.2 = (bf16[512,256]{1,0:T(8,128)(2,1)S(1)}, bf16[512,256]{1,0:T(8,128)(2,1)S(1)}, u32[]{:S(2)}, u32[]{:S(2)}) collective-permute-start(bf16[512,256]{1,0:T(8,128)(2,1)S(1)} %get-tuple-element.99), channel_id=1, source_target_pairs={{0,1},{1,0},{2,3},{3,2},{4,5},{5,4},{6,7},{7,6},{8,9},{9,8},{10,11... | collective-permute-start | bytes 786440 | tf_op jit(solution)/shard_map/ppermute | solution.py:227
  17.3 48.5 %collective-permute-start.16 = (bf16[2,8,256,256]{3,2,1,0:T(8,128)(2,1)S(1)}, bf16[2,8,256,256]{3,2,1,0:T(8,128)(2,1)}, u32[]{:S(2)}, u32[]{:S(2)}) collective-permute-start(bf16[2,8,256,256]{3,2,1,0:T(8,128)(2,1)S(1)} %bitcast.47), channel_id=1, source_target_pairs={{0,1},{1,0},{2,3},{3,2},{4,5},{5,4},{6,7},{7,6},{8,9},{9,8},{10,11... | collective-permute-start | bytes 6291464 | tf_op jit(solution)/shard_map/ppermute | solution.py:227
  20.4 10.5 %collective-permute-start.4 = (bf16[512,256]{1,0:T(8,128)(2,1)S(1)}, bf16[512,256]{1,0:T(8,128)(2,1)S(1)}, u32[]{:S(2)}, u32[]{:S(2)}) collective-permute-start(bf16[512,256]{1,0:T(8,128)(2,1)S(1)} %collective-permute-done.refs_2_), channel_id=1, source_target_pairs={{0,2},{2,4},{4,6},{6,8},{8,10},{10,12},{12,14},{14,0},{1,3},{3,5},... | collective-permute-start | bytes 786440 | tf_op jit(solution)/shard_map/ppermute | solution.py:232
  20.4 10.5 %collective-permute-start.5 = (bf16[512,256]{1,0:T(8,128)(2,1)S(1)}, bf16[512,256]{1,0:T(8,128)(2,1)S(1)}, u32[]{:S(2)}, u32[]{:S(2)}) collective-permute-start(bf16[512,256]{1,0:T(8,128)(2,1)S(1)} %collective-permute-done.1.refs_6_), channel_id=1, source_target_pairs={{0,14},{2,0},{4,2},{6,4},{8,6},{10,8},{12,10},{14,12},{1,15},{3,1}... | collective-permute-start | bytes 786440 | tf_op jit(solution)/shard_map/ppermute | solution.py:235
  23.6 10.2 %collective-permute-start.6 = (bf16[512,256]{1,0:T(8,128)(2,1)S(1)}, bf16[512,256]{1,0:T(8,128)(2,1)S(1)}, u32[]{:S(2)}, u32[]{:S(2)}) collective-permute-start(bf16[512,256]{1,0:T(8,128)(2,1)S(1)} %collective-permute-done.2.refs_9_), channel_id=1, source_target_pairs={{0,2},{2,4},{4,6},{6,8},{8,10},{10,12},{12,14},{14,0},{1,3},{3,5},... | collective-permute-start | bytes 786440 | tf_op jit(solution)/shard_map/ppermute | solution.py:232
  23.6 10.2 %collective-permute-start.7 = (bf16[512,256]{1,0:T(8,128)(2,1)S(1)}, bf16[512,256]{1,0:T(8,128)(2,1)S(1)}, u32[]{:S(2)}, u32[]{:S(2)}) collective-permute-start(bf16[512,256]{1,0:T(8,128)(2,1)S(1)} %collective-permute-done.2.refs_9_), channel_id=1, source_target_pairs={{0,14},{2,0},{4,2},{6,4},{8,6},{10,8},{12,10},{14,12},{1,15},{3,1}... | collective-permute-start | bytes 786440 | tf_op jit(solution)/shard_map/ppermute | solution.py:235
  33.8 9.9 %collective-permute-start.10 = (bf16[512,256]{1,0:T(8,128)(2,1)S(1)}, bf16[512,256]{1,0:T(8,128)(2,1)S(1)}, u32[]{:S(2)}, u32[]{:S(2)}) collective-permute-start(bf16[512,256]{1,0:T(8,128)(2,1)S(1)} %collective-permute-done.6.refs_10_), channel_id=1, source_target_pairs={{0,2},{2,4},{4,6},{6,8},{8,10},{10,12},{12,14},{14,0},{1,3},{3,5},... | collective-permute-start | bytes 786440 | tf_op jit(solution)/shard_map/ppermute | solution.py:232
  47.9 10.4 %collective-permute-start.13 = (bf16[512,256]{1,0:T(8,128)(2,1)S(1)}, bf16[512,256]{1,0:T(8,128)(2,1)S(1)}, u32[]{:S(2)}, u32[]{:S(2)}) collective-permute-start(bf16[512,256]{1,0:T(8,128)(2,1)S(1)} %collective-permute-done.10.refs_11_), channel_id=1, source_target_pairs={{0,2},{2,4},{4,6},{6,8},{8,10},{10,12},{12,14},{14,0},{1,3},{3,5},... | collective-permute-start | bytes 786440 | tf_op jit(solution)/shard_map/ppermute | solution.py:232
  65.8 27.8 %collective-permute-start.17 = (bf16[1,8,256,256]{3,2,1,0:T(8,128)(2,1)}, bf16[1,8,256,256]{3,2,1,0:T(8,128)(2,1)}, u32[]{:S(2)}, u32[]{:S(2)}) collective-permute-start(bf16[1,8,256,256]{3,2,1,0:T(8,128)(2,1)} %bitcast.14), channel_id=1, source_target_pairs={{0,1},{1,0},{2,3},{3,2},{4,5},{5,4},{6,7},{7,6},{8,9},{9,8},{10,11... | collective-permute-start | bytes 3145736 | tf_op jit(solution)/shard_map/ppermute | solution.py:227
  97.0 9.9 %collective-permute-start.27 = (bf16[1,8,256,256]{3,2,1,0:T(8,128)(2,1)}, bf16[1,8,256,256]{3,2,1,0:T(8,128)(2,1)S(1)}, u32[]{:S(2)}, u32[]{:S(2)}) collective-permute-start(bf16[1,8,256,256]{3,2,1,0:T(8,128)(2,1)} %collective-permute-done.17.refs_17_), channel_id=1, source_target_pairs={{0,16},{16,0},{1,17},{17,1},{2,18},{18,2},{3,19},{19,3},{4,20},{20... | collective-permute-start | bytes 3145736 | tf_op jit(solution)/shard_map/ppermute | solution.py:227
  97.0 27.1 %collective-permute-start.23 = (bf16[256,2048]{1,0:T(8,128)(2,1)S(1)}, bf16[256,2048]{1,0:T(8,128)(2,1)S(1)}, u32[]{:S(2)}, u32[]{:S(2)}) collective-permute-start(bf16[256,2048]{1,0:T(8,128)(2,1)S(1)} %constant_dynamic-slice_fusion.1), channel_id=1, source_target_pairs={{0,1},{1,0},{2,3},{3,2},{4,5},{5,4},{6,7},{7,6},{8,9},{9,8},{10,11... | collective-permute-start | bytes 3145736 | tf_op jit(solution)/shard_map/ppermute | solution.py:227
  102.0 11.8 %collective-permute-start.24 = (f32[16,512]{1,0:T(8,128)}, f32[16,512]{1,0:T(8,128)S(1)}, u32[]{:S(2)}, u32[]{:S(2)}) collective-permute-start(f32[16,512]{1,0:T(8,128)} %get-tuple-element.79), channel_id=1, source_target_pairs={{0,64},{64,128},{128,192},{192,0},{1,65},{65,129},{129,193},{193,1... | collective-permute-start | bytes 98312 | tf_op jit(solution)/shard_map/ppermute | solution.py:328
  103.6 10.2 %collective-permute-start.25 = (f32[16,512]{1,0:T(8,128)}, f32[16,512]{1,0:T(8,128)S(1)}, u32[]{:S(2)}, u32[]{:S(2)}) collective-permute-start(f32[16,512]{1,0:T(8,128)} %get-tuple-element.80), channel_id=1, source_target_pairs={{0,192},{64,0},{128,64},{192,128},{1,193},{65,1},{129,65},{193,129... | collective-permute-start | bytes 98312 | tf_op jit(solution)/shard_map/ppermute | solution.py:328
  104.0 9.8 %collective-permute-start.26 = (f32[16,512]{1,0:T(8,128)}, f32[16,512]{1,0:T(8,128)S(1)}, u32[]{:S(2)}, u32[]{:S(2)}) collective-permute-start(f32[16,512]{1,0:T(8,128)} %get-tuple-element.81), channel_id=1, source_target_pairs={{0,128},{64,192},{128,0},{192,64},{1,129},{65,193},{129,1},{193,65... | collective-permute-start | bytes 98312 | tf_op jit(solution)/shard_map/ppermute | solution.py:328
  131.7 10.8 %collective-permute-start.29 = (bf16[256,512]{1,0:T(8,128)(2,1)}, bf16[256,512]{1,0:T(8,128)(2,1)S(1)}, u32[]{:S(2)}, u32[]{:S(2)}) collective-permute-start(bf16[256,512]{1,0:T(8,128)(2,1)} %get-tuple-element.88), channel_id=1, source_target_pairs={{0,2},{2,4},{4,6},{6,8},{8,10},{10,12},{12,14},{14,0},{1,3},{3,5},... | collective-permute-start | bytes 786440 | tf_op jit(solution)/shard_map/ppermute | solution.py:232
  131.9 12.0 %collective-permute-start.33 = (bf16[256,512]{1,0:T(8,128)(2,1)}, bf16[256,512]{1,0:T(8,128)(2,1)S(1)}, u32[]{:S(2)}, u32[]{:S(2)}) collective-permute-start(bf16[256,512]{1,0:T(8,128)(2,1)} %get-tuple-element.92), channel_id=1, source_target_pairs={{0,14},{2,0},{4,2},{6,4},{8,6},{10,8},{12,10},{14,12},{1,15},{3,1}... | collective-permute-start | bytes 786440 | tf_op jit(solution)/shard_map/ppermute | solution.py:235
  143.8 14.7 %collective-permute-start.30 = (bf16[512,512]{1,0:T(8,128)(2,1)S(1)}, bf16[512,512]{1,0:T(8,128)(2,1)S(1)}, u32[]{:S(2)}, u32[]{:S(2)}) collective-permute-start(bf16[512,512]{1,0:T(8,128)(2,1)S(1)} %add_convert_fusion.6), channel_id=1, source_target_pairs={{0,2},{2,4},{4,6},{6,8},{8,10},{10,12},{12,14},{14,0},{1,3},{3,5},... | collective-permute-start | bytes 1572872 | tf_op jit(solution)/shard_map/ppermute | solution.py:232
  145.1 13.9 %collective-permute-start.34 = (bf16[512,512]{1,0:T(8,128)(2,1)S(1)}, bf16[512,512]{1,0:T(8,128)(2,1)S(1)}, u32[]{:S(2)}, u32[]{:S(2)}) collective-permute-start(bf16[512,512]{1,0:T(8,128)(2,1)S(1)} %add_convert_fusion.3), channel_id=1, source_target_pairs={{0,14},{2,0},{4,2},{6,4},{8,6},{10,8},{12,10},{14,12},{1,15},{3,1}... | collective-permute-start | bytes 1572872 | tf_op jit(solution)/shard_map/ppermute | solution.py:235
  158.6 13.8 %collective-permute-start.31 = (bf16[512,512]{1,0:T(8,128)(2,1)S(1)}, bf16[512,512]{1,0:T(8,128)(2,1)S(1)}, u32[]{:S(2)}, u32[]{:S(2)}) collective-permute-start(bf16[512,512]{1,0:T(8,128)(2,1)S(1)} %add_convert_fusion.5), channel_id=1, source_target_pairs={{0,2},{2,4},{4,6},{6,8},{8,10},{10,12},{12,14},{14,0},{1,3},{3,5},... | collective-permute-start | bytes 1572872 | tf_op jit(solution)/shard_map/ppermute | solution.py:232
  159.2 13.5 %collective-permute-start.35 = (bf16[512,512]{1,0:T(8,128)(2,1)S(1)}, bf16[512,512]{1,0:T(8,128)(2,1)S(1)}, u32[]{:S(2)}, u32[]{:S(2)}) collective-permute-start(bf16[512,512]{1,0:T(8,128)(2,1)S(1)} %add_convert_fusion.2), channel_id=1, source_target_pairs={{0,14},{2,0},{4,2},{6,4},{8,6},{10,8},{12,10},{14,12},{1,15},{3,1}... | collective-permute-start | bytes 1572872 | tf_op jit(solution)/shard_map/ppermute | solution.py:235
  172.6 12.9 %collective-permute-start.32 = (bf16[512,512]{1,0:T(8,128)(2,1)S(1)}, bf16[512,512]{1,0:T(8,128)(2,1)S(1)}, u32[]{:S(2)}, u32[]{:S(2)}) collective-permute-start(bf16[512,512]{1,0:T(8,128)(2,1)S(1)} %add_convert_fusion.4), channel_id=1, source_target_pairs={{0,2},{2,4},{4,6},{6,8},{8,10},{10,12},{12,14},{14,0},{1,3},{3,5},... | collective-permute-start | bytes 1572872 | tf_op jit(solution)/shard_map/ppermute | solution.py:232
  172.8 12.6 %collective-permute-start.36 = (bf16[512,512]{1,0:T(8,128)(2,1)S(1)}, bf16[512,512]{1,0:T(8,128)(2,1)S(1)}, u32[]{:S(2)}, u32[]{:S(2)}) collective-permute-start(bf16[512,512]{1,0:T(8,128)(2,1)S(1)} %add_convert_fusion.1), channel_id=1, source_target_pairs={{0,14},{2,0},{4,2},{6,4},{8,6},{10,8},{12,10},{14,12},{1,15},{3,1}... | collective-permute-start | bytes 1572872 | tf_op jit(solution)/shard_map/ppermute | solution.py:235
  (49 other events, 752.6 us)

commit v2 on v1

--- a/solution.py
+++ b/solution.py
@@ -237,11 +237,35 @@
     half, blocks = features // 2, features // 2 // width
     at = core * half
     mixed_part = lax.dynamic_slice(in_weight, (1, at, 0), (2, half, width)).reshape(2, blocks, width, width)
+    chunk_at = [((z + o) % n_z) * 2 + xh for o in (0, -1, -2, -3, -4, 1, 2, 3)]
+    chunk_at += [((z + o) % n_z) * 2 + 1 - xh for o in (0, -1, -2, -3, 1, 2, 3, 4)]
+    part_at = [core * blocks, (1 - core) * blocks]
+    where = jnp.stack(chunk_at + part_at).astype(jnp.int32)
+    reach = [4, -3, 3, 2, -2, 1, -1, 0]
+    where_out = jnp.stack([core, 1 - core] + [(z + r) % n_z for r in reach]).astype(jnp.int32)
+
+    slots = jnp.stack(
+        [
+            8 * y + 4 * (xl ^ dl) + 2 * (core ^ dc) + (xh ^ dh)
+            for dl, dh in ((0, 0), (1, 0), (0, 1), (1, 1))
+            for dc in (0, 1)
+        ]
+    )
+    ahead = [0, 1, -1, 2]
+    targets = jnp.stack([8 * ((y + o) % n_y) + 4 * xl + 2 * core + xh for o in ahead])
+    names = jnp.arange(block_order.shape[0])
+
+    def place_of(which):
+        return jnp.sum(jnp.where(names[None] == which[:, None], block_order[None], 0), axis=1)
+
+    lags = ((place_of(targets)[:, None] - 1 - place_of(slots)[None]) * tokens).astype(F32).reshape(-1)
     of1, ob1, p0, small_peer, mixed_part = together(
         (ahead_z(mine), back_z(mine), swap(others), swap(small), mixed_part)
     )
     mixed_part = swap(mixed_part)
-    of2, ob2, pf1, pb1 = together((ahead_z(of1), back_z(ob1), ahead_z(p0), back_z(p0)))
+    of2, ob2, pf1, pb1, where, where_out, lags = together(
+        (ahead_z(of1), back_z(ob1), ahead_z(p0), back_z(p0), where, where_out, lags)
+    )
     of3, ob3, pf2, pb2 = together((ahead_z(of2), back_z(ob2), ahead_z(pf1), back_z(pb1)))
     of4, pf3, pb3, at = together((ahead_z(of3), ahead_z(pf2), back_z(pb2), at))
     query_part = lax.dynamic_slice(in_weight, (0, at, 0), (1, half, width)).reshape(1, blocks, width, width)
@@ -252,13 +276,6 @@
     small = jnp.concatenate([small, small_peer], 1)
     rates, gains, skip = small[:ORDER], small[ORDER : 2 * ORDER], small[2 * ORDER :]
     chunks = [mine, of1, of2, of3, of4, ob1, ob2, ob3, p0, pf1, pf2, pf3, pb1, pb2, pb3, pb4]
-    chunk_at = [((z + o) % n_z) * 2 + xh for o in (0, -1, -2, -3, -4, 1, 2, 3)]
-    chunk_at += [((z + o) % n_z) * 2 + 1 - xh for o in (0, -1, -2, -3, 1, 2, 3, 4)]
-    part_at = [core * blocks, (1 - core) * blocks]
-    where = jnp.stack(chunk_at + part_at).astype(jnp.int32)
-    reach = [4, -3, 3, 2, -2, 1, -1, 0]
-    where_out = jnp.stack([core, 1 - core] + [(z + r) % n_z for r in reach]).astype(jnp.int32)
-
     params = pltpu.CompilerParams(vmem_limit_bytes=60 << 20)
     mixed, ends, state, query_own = pl.pallas_call(
         lambda *refs: project_all(*refs, n_chunks=len(chunks)),
@@ -304,21 +321,6 @@
         ],
         compiler_params=params,
     )(where, *chunks, query_part, swap(query_part, "core"))
-    slots = jnp.stack(
-        [
-            8 * y + 4 * (xl ^ dl) + 2 * (core ^ dc) + (xh ^ dh)
-            for dl, dh in ((0, 0), (1, 0), (0, 1), (1, 1))
-            for dc in (0, 1)
-        ]
-    )
-    ahead = [0, 1, -1, 2]
-    targets = jnp.stack([8 * ((y + o) % n_y) + 4 * xl + 2 * core + xh for o in ahead])
-    names = jnp.arange(block_order.shape[0])
-
-    def place_of(which):
-        return jnp.sum(jnp.where(names[None] == which[:, None], block_order[None], 0), axis=1)
-
-    lags = ((place_of(targets)[:, None] - 1 - place_of(slots)[None]) * tokens).astype(F32).reshape(-1)
     given = pl.pallas_call(
         lambda *refs: pass_on(*refs, n_pieces=len(pieces)),
         in_specs=[SMEM] + [VMEM] * (len(pieces) + 1),

time: 195 us -> 195 us (level)
    ppermute x9, waiting for transfers between devices: 16.1 us -> 19.8 us  [swap(): return lax.ppermute(piece, axis, SWAP)]
    ppermute x11, waiting for transfers between devices: 48.7 us -> 46.5 us  [ahead_z(): return lax.ppermute(x, 'z', around(n_z, 1))]
    unnamed x70 -> x66, local copies, waits for them, and re-layouts: 5.34 us -> 5.33 us
  transfers between devices with their start and end apart: 38 -> 38, of which waited for: 21 -> 20; matrix products, arithmetic and copies ran while one was open for 7% -> 7% of each run, Pallas kernels for 19% -> 19%
where the time goes in v2:
time: 195 us
  waiting for transfers between devices  73.2 us (38%)
  starting transfers between devices  59.6 us (31%)
  Pallas kernels  40.2 us (21%)
  local copies, waits for them, and re-layouts  13.7 us (7%)
  other arithmetic  7.44 us (4%)
    ppermute x11, waiting for transfers between devices, ahead_z(): return lax.ppermute(x, 'z', around(n_z, 1))  46.5 us
    ppermute x11, starting transfers between devices, back_z(): return lax.ppermute(x, 'z', around(n_z, -1))  33.3 us
    ppermute x9, waiting for transfers between devices, swap(): return lax.ppermute(piece, axis, SWAP)  19.8 us
    pallas_call x1, Pallas kernels, per_device(): pl.pallas_call(lambda *refs: project_all(*refs, n_chunks=len(chunks)), in...  13.9 us
    ppermute x9, starting transfers between devices, swap(): return lax.ppermute(piece, axis, SWAP)  12 us
    pallas_call x2, Pallas kernels, project_cols(): pl.pallas_call(lambda *refs: project_out(*refs, first=first, n_parts=len(...  11.5 us
    pallas_call x1, Pallas kernels, per_device(): pl.pallas_call(lambda *refs: convolve(*refs, n_given=len(given)), in_spec...  7.17 us
    ppermute x11, starting transfers between devices, ahead_z(): return lax.ppermute(x, 'z', around(n_z, 1))  6.13 us
  transfers between devices with their start and end apart: 38, of which 20 were waited for; matrix products, arithmetic and copies ran while one was open for 7% of the time, Pallas kernels for 19%

profile of v2, /device:TPU:8, one launch (start us, length us, event | category | flops | bytes accessed | tf_op | source)
XLA Modules:
  0.0 194.8 jit_solution(15025592181128731149)
XLA Ops:
  3.1 4.0 %collective-permute-start.1 = (bf16[512,256]{1,0:T(8,128)(2,1)S(1)}, bf16[512,256]{1,0:T(8,128)(2,1)S(1)}, u32[]{:S(2)}, u32[]{:S(2)}) collective-permute-start(bf16[512,256]{1,0:T(8,128)(2,1)S(1)} %get-tuple-element.106.refs_1_), channel_id=1, source_target_pairs={{0,14},{2,0},{4,2},{6,4},{8,6},{10,8},{12,10},{14,12},{1,15},{3,1}... | collective-permute-start | bytes 786440 | tf_op jit(solution)/shard_map/ppermute | solution.py:235
  7.1 3.0 %collective-permute-start.2 = (bf16[512,256]{1,0:T(8,128)(2,1)S(1)}, bf16[512,256]{1,0:T(8,128)(2,1)S(1)}, u32[]{:S(2)}, u32[]{:S(2)}) collective-permute-start(bf16[512,256]{1,0:T(8,128)(2,1)S(1)} %get-tuple-element.105), channel_id=1, source_target_pairs={{0,1},{1,0},{2,3},{3,2},{4,5},{5,4},{6,7},{7,6},{8,9},{9,8},{10,11... | collective-permute-start | bytes 786440 | tf_op jit(solution)/shard_map/ppermute | solution.py:227
  13.2 4.1 %collective-permute-done.3 = f32[33,256]{1,0:T(8,128)S(1)} collective-permute-done((f32[33,256]{1,0:T(8,128)S(1)}, f32[33,256]{1,0:T(8,128)S(1)}, u32[]{:S(2)}, u32[]{:S(2)}) %collective-permute-start.3) | collective-permute-done | bytes 33824 | tf_op jit(solution)/shard_map/ppermute | solution.py:227
  17.3 3.1 %collective-permute-start.16 = (bf16[2,8,256,256]{3,2,1,0:T(8,128)(2,1)S(1)}, bf16[2,8,256,256]{3,2,1,0:T(8,128)(2,1)}, u32[]{:S(2)}, u32[]{:S(2)}) collective-permute-start(bf16[2,8,256,256]{3,2,1,0:T(8,128)(2,1)S(1)} %bitcast.47), channel_id=1, source_target_pairs={{0,1},{1,0},{2,3},{3,2},{4,5},{5,4},{6,7},{7,6},{8,9},{9,8},{10,11... | collective-permute-start | bytes 6291464 | tf_op jit(solution)/shard_map/ppermute | solution.py:227
  20.8 3.2 %collective-permute-start.7 = (bf16[512,256]{1,0:T(8,128)(2,1)S(1)}, bf16[512,256]{1,0:T(8,128)(2,1)S(1)}, u32[]{:S(2)}, u32[]{:S(2)}) collective-permute-start(bf16[512,256]{1,0:T(8,128)(2,1)S(1)} %collective-permute-done.2.refs_9_), channel_id=1, source_target_pairs={{0,14},{2,0},{4,2},{6,4},{8,6},{10,8},{12,10},{14,12},{1,15},{3,1}... | collective-permute-start | bytes 786440 | tf_op jit(solution)/shard_map/ppermute | solution.py:235
  24.1 3.2 %collective-permute-start.5 = (bf16[512,256]{1,0:T(8,128)(2,1)S(1)}, bf16[512,256]{1,0:T(8,128)(2,1)}, u32[]{:S(2)}, u32[]{:S(2)}) collective-permute-start(bf16[512,256]{1,0:T(8,128)(2,1)S(1)} %collective-permute-done.1.refs_6_), channel_id=1, source_target_pairs={{0,14},{2,0},{4,2},{6,4},{8,6},{10,8},{12,10},{14,12},{1,15},{3,1}... | collective-permute-start | bytes 786440 | tf_op jit(solution)/shard_map/ppermute | solution.py:235
  29.6 4.7 %collective-permute-done.4.refs_3_ = bf16[512,256]{1,0:T(8,128)(2,1)} collective-permute-done((bf16[512,256]{1,0:T(8,128)(2,1)S(1)}, bf16[512,256]{1,0:T(8,128)(2,1)}, u32[]{:S(2)}, u32[]{:S(2)}) %collective-permute-start.4) | collective-permute-done | bytes 262176 | tf_op jit(solution)/shard_map/ppermute | solution.py:232
  34.5 3.2 %collective-permute-start.11 = (bf16[512,256]{1,0:T(8,128)(2,1)S(1)}, bf16[512,256]{1,0:T(8,128)(2,1)S(1)}, u32[]{:S(2)}, u32[]{:S(2)}) collective-permute-start(bf16[512,256]{1,0:T(8,128)(2,1)S(1)} %collective-permute-done.7.refs_13_), channel_id=1, source_target_pairs={{0,14},{2,0},{4,2},{6,4},{8,6},{10,8},{12,10},{14,12},{1,15},{3,1}... | collective-permute-start | bytes 786440 | tf_op jit(solution)/shard_map/ppermute | solution.py:235
  37.7 3.2 %collective-permute-start.9 = (bf16[512,256]{1,0:T(8,128)(2,1)}, bf16[512,256]{1,0:T(8,128)(2,1)S(1)}, u32[]{:S(2)}, u32[]{:S(2)}) collective-permute-start(bf16[512,256]{1,0:T(8,128)(2,1)} %collective-permute-done.5.refs_7_), channel_id=1, source_target_pairs={{0,14},{2,0},{4,2},{6,4},{8,6},{10,8},{12,10},{14,12},{1,15},{3,1}... | collective-permute-start | bytes 786440 | tf_op jit(solution)/shard_map/ppermute | solution.py:235
  40.9 3.3 %collective-permute-done.10.refs_11_ = bf16[512,256]{1,0:T(8,128)(2,1)S(1)} collective-permute-done((bf16[512,256]{1,0:T(8,128)(2,1)S(1)}, bf16[512,256]{1,0:T(8,128)(2,1)S(1)}, u32[]{:S(2)}, u32[]{:S(2)}) %collective-permute-start.10) | collective-permute-done | bytes 262176 | tf_op jit(solution)/shard_map/ppermute | solution.py:232
  51.7 4.5 %collective-permute-done.12.refs_5_ = bf16[512,256]{1,0:T(8,128)(2,1)S(1)} collective-permute-done((bf16[512,256]{1,0:T(8,128)(2,1)S(1)}, bf16[512,256]{1,0:T(8,128)(2,1)S(1)}, u32[]{:S(2)}, u32[]{:S(2)}) %collective-permute-start.12) | collective-permute-done | bytes 262176 | tf_op jit(solution)/shard_map/ppermute | solution.py:232
  72.1 13.9 %shard_map.73 = (bf16[512,512]{1,0:T(8,128)(2,1)}, f32[16,8,512]{2,1,0:T(8,128)}, f32[16,512]{1,0:T(8,128)}, bf16[512,256]{1,0:T(8,128)(2,1)}) custom-call(s32[18]{0:T(128)} %stack.159.refs_0_, bf16[512,256]{1,0:T(8,128)(2,1)} %copy-done.3, bf16[512,256]{1,0:T(8,128)(2,1)} %copy-done.5, bf16[512,256]{1,0:T(8,128)(2,1)} %collective-permute-done.4.refs_3_, ...), custom_call_target="tpu_custom_call" | custom-call | tf_op jit(solution)/shard_map/pallas_call | solution.py:280
  106.7 5.9 %shard_map.75.refs_7_ = bf16[512,256]{1,0:T(8,128)(2,1)} custom-call(s32[18]{0:T(128)} %stack.159.refs_0_, bf16[512,256]{1,0:T(8,128)(2,1)} %copy-done.3, bf16[512,256]{1,0:T(8,128)(2,1)} %copy-done.5, bf16[512,256]{1,0:T(8,128)(2,1)} %collective-permute-done.4.refs_3_, bf16[512,256]{1,0:T(8,128)(2,1)} %copy-done.12, bf16[512,256]{1,0:T(8,128)(2,1)} %copy-done.14, ...), custom_call_target="tpu_custom_call" | custom-call | tf_op jit(solution)/shard_map/pallas_call | solution.py:312
  113.2 7.2 %shard_map.76.refs_1_ = bf16[512,512]{1,0:T(8,128)(2,1)} custom-call(f32[16,512]{1,0:T(8,128)} %get-tuple-element.84.refs_0_, f32[16,512]{1,0:T(8,128)} %copy-done.28, f32[16,512]{1,0:T(8,128)} %copy-done.29, f32[16,512]{1,0:T(8,128)} %copy-done.30, f32[16,8,512]{2,1,0:T(8,128)} %get-tuple-element.88.refs_4_, bf16[512,512]{1,0:T(8,128)(2,1)} %get-tuple-element.89.refs_5_, ...), custom_call_target="tpu_custom_call" | custom-call | tf_op jit(solution)/shard_map/pallas_call | solution.py:332
  120.4 3.9 %collective-permute-done.23.refs_3_ = bf16[256,2048]{1,0:T(8,128)(2,1)S(1)} collective-permute-done((bf16[256,2048]{1,0:T(8,128)(2,1)S(1)}, bf16[256,2048]{1,0:T(8,128)(2,1)S(1)}, u32[]{:S(2)}, u32[]{:S(2)}) %collective-permute-start.23) | collective-permute-done | bytes 1048608 | tf_op jit(solution)/shard_map/ppermute | solution.py:227
  127.9 3.9 %shard_map.77 = (bf16[256,512]{1,0:T(8,128)(2,1)}, bf16[256,512]{1,0:T(8,128)(2,1)}) custom-call(s32[10]{0:T(128)} %stack.170.refs_0_, bf16[512,512]{1,0:T(8,128)(2,1)} %shard_map.76.refs_1_, bf16[256,4096]{1,0:T(8,128)(2,1)} %refs_2_.3, bf16[256,2048]{1,0:T(8,128)(2,1)} %copy-done.1, bf16[256,2048]{1,0:T(8,128)(2,1)} %copy-done.2), custom_call_target="tpu_custom_call" | custom-call | tf_op jit(solution)/shard_map/pallas_call | solution.py:344
  135.2 7.5 %shard_map.78 = (bf16[512,512]{1,0:T(8,128)(2,1)}, bf16[512,512]{1,0:T(8,128)(2,1)}, bf16[512,512]{1,0:T(8,128)(2,1)}, bf16[512,512]{1,0:T(8,128)(2,1)}, bf16[51...) custom-call(s32[10]{0:T(128)} %stack.170.refs_0_, bf16[512,512]{1,0:T(8,128)(2,1)} %shard_map.76.refs_1_, ...), custom_call_target="tpu_custom_call" | custom-call | tf_op jit(solution)/shard_map/pallas_call | solution.py:344
  145.3 3.3 %collective-permute-start.34 = (bf16[512,512]{1,0:T(8,128)(2,1)S(1)}, bf16[512,512]{1,0:T(8,128)(2,1)S(1)}, u32[]{:S(2)}, u32[]{:S(2)}) collective-permute-start(bf16[512,512]{1,0:T(8,128)(2,1)S(1)} %add_convert_fusion.3), channel_id=1, source_target_pairs={{0,14},{2,0},{4,2},{6,4},{8,6},{10,8},{12,10},{14,12},{1,15},{3,1}... | collective-permute-start | bytes 1572872 | tf_op jit(solution)/shard_map/ppermute | solution.py:235
  148.5 10.1 %collective-permute-done.30 = bf16[512,512]{1,0:T(8,128)(2,1)S(1)} collective-permute-done((bf16[512,512]{1,0:T(8,128)(2,1)S(1)}, bf16[512,512]{1,0:T(8,128)(2,1)S(1)}, u32[]{:S(2)}, u32[]{:S(2)}) %collective-permute-start.30) | collective-permute-done | bytes 524320 | tf_op jit(solution)/shard_map/ppermute | solution.py:232
  159.3 3.8 %collective-permute-start.35 = (bf16[512,512]{1,0:T(8,128)(2,1)S(1)}, bf16[512,512]{1,0:T(8,128)(2,1)S(1)}, u32[]{:S(2)}, u32[]{:S(2)}) collective-permute-start(bf16[512,512]{1,0:T(8,128)(2,1)S(1)} %add_convert_fusion.2), channel_id=1, source_target_pairs={{0,14},{2,0},{4,2},{6,4},{8,6},{10,8},{12,10},{14,12},{1,15},{3,1}... | collective-permute-start | bytes 1572872 | tf_op jit(solution)/shard_map/ppermute | solution.py:235
  163.1 9.5 %collective-permute-done.31 = bf16[512,512]{1,0:T(8,128)(2,1)S(1)} collective-permute-done((bf16[512,512]{1,0:T(8,128)(2,1)S(1)}, bf16[512,512]{1,0:T(8,128)(2,1)S(1)}, u32[]{:S(2)}, u32[]{:S(2)}) %collective-permute-start.31) | collective-permute-done | bytes 524320 | tf_op jit(solution)/shard_map/ppermute | solution.py:232
  173.0 3.7 %collective-permute-start.36 = (bf16[512,512]{1,0:T(8,128)(2,1)S(1)}, bf16[512,512]{1,0:T(8,128)(2,1)S(1)}, u32[]{:S(2)}, u32[]{:S(2)}) collective-permute-start(bf16[512,512]{1,0:T(8,128)(2,1)S(1)} %add_convert_fusion.1), channel_id=1, source_target_pairs={{0,14},{2,0},{4,2},{6,4},{8,6},{10,8},{12,10},{14,12},{1,15},{3,1}... | collective-permute-start | bytes 1572872 | tf_op jit(solution)/shard_map/ppermute | solution.py:235
  176.7 8.9 %collective-permute-done.32 = bf16[512,512]{1,0:T(8,128)(2,1)S(1)} collective-permute-done((bf16[512,512]{1,0:T(8,128)(2,1)S(1)}, bf16[512,512]{1,0:T(8,128)(2,1)S(1)}, u32[]{:S(2)}, u32[]{:S(2)}) %collective-permute-start.32) | collective-permute-done | bytes 524320 | tf_op jit(solution)/shard_map/ppermute | solution.py:232
  187.6 6.2 %collective-permute-done.37 = bf16[512,256]{1,0:T(8,128)(2,1)S(1)} collective-permute-done((bf16[512,256]{1,0:T(8,128)(2,1)S(1)}, bf16[512,256]{1,0:T(8,128)(2,1)S(1)}, u32[]{:S(2)}, u32[]{:S(2)}) %collective-permute-start.37) | collective-permute-done | bytes 262176 | tf_op jit(solution)/shard_map/ppermute | solution.py:227
  (154 shorter events, 66.8 us)
Async XLA Ops:
  1.1 16.2 %collective-permute-start = (bf16[512,256]{1,0:T(8,128)(2,1)S(1)}, bf16[512,256]{1,0:T(8,128)(2,1)S(1)}, u32[]{:S(2)}, u32[]{:S(2)}) collective-permute-start(bf16[512,256]{1,0:T(8,128)(2,1)S(1)} %get-tuple-element.106.refs_1_), channel_id=1, source_target_pairs={{0,2},{2,4},{4,6},{6,8},{8,10},{10,12},{12,14},{14,0},{1,3},{3,5},... | collective-permute-start | bytes 786440 | tf_op jit(solution)/shard_map/ppermute | solution.py:232
  3.1 14.2 %collective-permute-start.1 = (bf16[512,256]{1,0:T(8,128)(2,1)S(1)}, bf16[512,256]{1,0:T(8,128)(2,1)S(1)}, u32[]{:S(2)}, u32[]{:S(2)}) collective-permute-start(bf16[512,256]{1,0:T(8,128)(2,1)S(1)} %get-tuple-element.106.refs_1_), channel_id=1, source_target_pairs={{0,14},{2,0},{4,2},{6,4},{8,6},{10,8},{12,10},{14,12},{1,15},{3,1}... | collective-permute-start | bytes 786440 | tf_op jit(solution)/shard_map/ppermute | solution.py:235
  7.1 10.2 %collective-permute-start.2 = (bf16[512,256]{1,0:T(8,128)(2,1)S(1)}, bf16[512,256]{1,0:T(8,128)(2,1)S(1)}, u32[]{:S(2)}, u32[]{:S(2)}) collective-permute-start(bf16[512,256]{1,0:T(8,128)(2,1)S(1)} %get-tuple-element.105), channel_id=1, source_target_pairs={{0,1},{1,0},{2,3},{3,2},{4,5},{5,4},{6,7},{7,6},{8,9},{9,8},{10,11... | collective-permute-start | bytes 786440 | tf_op jit(solution)/shard_map/ppermute | solution.py:227
  17.3 49.1 %collective-permute-start.16 = (bf16[2,8,256,256]{3,2,1,0:T(8,128)(2,1)S(1)}, bf16[2,8,256,256]{3,2,1,0:T(8,128)(2,1)}, u32[]{:S(2)}, u32[]{:S(2)}) collective-permute-start(bf16[2,8,256,256]{3,2,1,0:T(8,128)(2,1)S(1)} %bitcast.47), channel_id=1, source_target_pairs={{0,1},{1,0},{2,3},{3,2},{4,5},{5,4},{6,7},{7,6},{8,9},{9,8},{10,11... | collective-permute-start | bytes 6291464 | tf_op jit(solution)/shard_map/ppermute | solution.py:227
  20.8 13.6 %collective-permute-start.6 = (bf16[512,256]{1,0:T(8,128)(2,1)S(1)}, bf16[512,256]{1,0:T(8,128)(2,1)S(1)}, u32[]{:S(2)}, u32[]{:S(2)}) collective-permute-start(bf16[512,256]{1,0:T(8,128)(2,1)S(1)} %collective-permute-done.2.refs_9_), channel_id=1, source_target_pairs={{0,2},{2,4},{4,6},{6,8},{8,10},{10,12},{12,14},{14,0},{1,3},{3,5},... | collective-permute-start | bytes 786440 | tf_op jit(solution)/shard_map/ppermute | solution.py:232
  20.8 13.5 %collective-permute-start.7 = (bf16[512,256]{1,0:T(8,128)(2,1)S(1)}, bf16[512,256]{1,0:T(8,128)(2,1)S(1)}, u32[]{:S(2)}, u32[]{:S(2)}) collective-permute-start(bf16[512,256]{1,0:T(8,128)(2,1)S(1)} %collective-permute-done.2.refs_9_), channel_id=1, source_target_pairs={{0,14},{2,0},{4,2},{6,4},{8,6},{10,8},{12,10},{14,12},{1,15},{3,1}... | collective-permute-start | bytes 786440 | tf_op jit(solution)/shard_map/ppermute | solution.py:235
  24.1 10.3 %collective-permute-start.4 = (bf16[512,256]{1,0:T(8,128)(2,1)S(1)}, bf16[512,256]{1,0:T(8,128)(2,1)}, u32[]{:S(2)}, u32[]{:S(2)}) collective-permute-start(bf16[512,256]{1,0:T(8,128)(2,1)S(1)} %collective-permute-done.refs_2_), channel_id=1, source_target_pairs={{0,2},{2,4},{4,6},{6,8},{8,10},{10,12},{12,14},{14,0},{1,3},{3,5},... | collective-permute-start | bytes 786440 | tf_op jit(solution)/shard_map/ppermute | solution.py:232
  24.1 10.3 %collective-permute-start.5 = (bf16[512,256]{1,0:T(8,128)(2,1)S(1)}, bf16[512,256]{1,0:T(8,128)(2,1)}, u32[]{:S(2)}, u32[]{:S(2)}) collective-permute-start(bf16[512,256]{1,0:T(8,128)(2,1)S(1)} %collective-permute-done.1.refs_6_), channel_id=1, source_target_pairs={{0,14},{2,0},{4,2},{6,4},{8,6},{10,8},{12,10},{14,12},{1,15},{3,1}... | collective-permute-start | bytes 786440 | tf_op jit(solution)/shard_map/ppermute | solution.py:235
  34.4 9.8 %collective-permute-start.10 = (bf16[512,256]{1,0:T(8,128)(2,1)S(1)}, bf16[512,256]{1,0:T(8,128)(2,1)S(1)}, u32[]{:S(2)}, u32[]{:S(2)}) collective-permute-start(bf16[512,256]{1,0:T(8,128)(2,1)S(1)} %collective-permute-done.6.refs_10_), channel_id=1, source_target_pairs={{0,2},{2,4},{4,6},{6,8},{8,10},{10,12},{12,14},{14,0},{1,3},{3,5},... | collective-permute-start | bytes 786440 | tf_op jit(solution)/shard_map/ppermute | solution.py:232
  34.5 9.7 %collective-permute-start.11 = (bf16[512,256]{1,0:T(8,128)(2,1)S(1)}, bf16[512,256]{1,0:T(8,128)(2,1)S(1)}, u32[]{:S(2)}, u32[]{:S(2)}) collective-permute-start(bf16[512,256]{1,0:T(8,128)(2,1)S(1)} %collective-permute-done.7.refs_13_), channel_id=1, source_target_pairs={{0,14},{2,0},{4,2},{6,4},{8,6},{10,8},{12,10},{14,12},{1,15},{3,1}... | collective-permute-start | bytes 786440 | tf_op jit(solution)/shard_map/ppermute | solution.py:235
  48.4 10.5 %collective-permute-start.13 = (bf16[512,256]{1,0:T(8,128)(2,1)S(1)}, bf16[512,256]{1,0:T(8,128)(2,1)S(1)}, u32[]{:S(2)}, u32[]{:S(2)}) collective-permute-start(bf16[512,256]{1,0:T(8,128)(2,1)S(1)} %collective-permute-done.10.refs_11_), channel_id=1, source_target_pairs={{0,2},{2,4},{4,6},{6,8},{8,10},{10,12},{12,14},{14,0},{1,3},{3,5},... | collective-permute-start | bytes 786440 | tf_op jit(solution)/shard_map/ppermute | solution.py:232
  66.4 27.8 %collective-permute-start.17 = (bf16[1,8,256,256]{3,2,1,0:T(8,128)(2,1)}, bf16[1,8,256,256]{3,2,1,0:T(8,128)(2,1)}, u32[]{:S(2)}, u32[]{:S(2)}) collective-permute-start(bf16[1,8,256,256]{3,2,1,0:T(8,128)(2,1)} %bitcast.44), channel_id=1, source_target_pairs={{0,1},{1,0},{2,3},{3,2},{4,5},{5,4},{6,7},{7,6},{8,9},{9,8},{10,11... | collective-permute-start | bytes 3145736 | tf_op jit(solution)/shard_map/ppermute | solution.py:227
  97.2 27.1 %collective-permute-start.23 = (bf16[256,2048]{1,0:T(8,128)(2,1)S(1)}, bf16[256,2048]{1,0:T(8,128)(2,1)S(1)}, u32[]{:S(2)}, u32[]{:S(2)}) collective-permute-start(bf16[256,2048]{1,0:T(8,128)(2,1)S(1)} %constant_dynamic-slice_fusion.1), channel_id=1, source_target_pairs={{0,1},{1,0},{2,3},{3,2},{4,5},{5,4},{6,7},{7,6},{8,9},{9,8},{10,11... | collective-permute-start | bytes 3145736 | tf_op jit(solution)/shard_map/ppermute | solution.py:227
  100.7 11.8 %collective-permute-start.24 = (f32[16,512]{1,0:T(8,128)}, f32[16,512]{1,0:T(8,128)S(1)}, u32[]{:S(2)}, u32[]{:S(2)}) collective-permute-start(f32[16,512]{1,0:T(8,128)} %get-tuple-element.85), channel_id=1, source_target_pairs={{0,64},{64,128},{128,192},{192,0},{1,65},{65,129},{129,193},{193,1... | collective-permute-start | bytes 98312 | tf_op jit(solution)/shard_map/ppermute | solution.py:330
  102.3 10.3 %collective-permute-start.25 = (f32[16,512]{1,0:T(8,128)}, f32[16,512]{1,0:T(8,128)S(1)}, u32[]{:S(2)}, u32[]{:S(2)}) collective-permute-start(f32[16,512]{1,0:T(8,128)} %get-tuple-element.86), channel_id=1, source_target_pairs={{0,192},{64,0},{128,64},{192,128},{1,193},{65,1},{129,65},{193,129... | collective-permute-start | bytes 98312 | tf_op jit(solution)/shard_map/ppermute | solution.py:330
  102.8 9.8 %collective-permute-start.26 = (f32[16,512]{1,0:T(8,128)}, f32[16,512]{1,0:T(8,128)S(1)}, u32[]{:S(2)}, u32[]{:S(2)}) collective-permute-start(f32[16,512]{1,0:T(8,128)} %get-tuple-element.87), channel_id=1, source_target_pairs={{0,128},{64,192},{128,0},{192,64},{1,129},{65,193},{129,1},{193,65... | collective-permute-start | bytes 98312 | tf_op jit(solution)/shard_map/ppermute | solution.py:330
  131.9 10.8 %collective-permute-start.29 = (bf16[256,512]{1,0:T(8,128)(2,1)}, bf16[256,512]{1,0:T(8,128)(2,1)S(1)}, u32[]{:S(2)}, u32[]{:S(2)}) collective-permute-start(bf16[256,512]{1,0:T(8,128)(2,1)} %get-tuple-element.94), channel_id=1, source_target_pairs={{0,2},{2,4},{4,6},{6,8},{8,10},{10,12},{12,14},{14,0},{1,3},{3,5},... | collective-permute-start | bytes 786440 | tf_op jit(solution)/shard_map/ppermute | solution.py:232
  132.5 11.6 %collective-permute-start.33 = (bf16[256,512]{1,0:T(8,128)(2,1)}, bf16[256,512]{1,0:T(8,128)(2,1)S(1)}, u32[]{:S(2)}, u32[]{:S(2)}) collective-permute-start(bf16[256,512]{1,0:T(8,128)(2,1)} %get-tuple-element.98), channel_id=1, source_target_pairs={{0,14},{2,0},{4,2},{6,4},{8,6},{10,8},{12,10},{14,12},{1,15},{3,1}... | collective-permute-start | bytes 786440 | tf_op jit(solution)/shard_map/ppermute | solution.py:235
  144.0 14.7 %collective-permute-start.30 = (bf16[512,512]{1,0:T(8,128)(2,1)S(1)}, bf16[512,512]{1,0:T(8,128)(2,1)S(1)}, u32[]{:S(2)}, u32[]{:S(2)}) collective-permute-start(bf16[512,512]{1,0:T(8,128)(2,1)S(1)} %add_convert_fusion.6), channel_id=1, source_target_pairs={{0,2},{2,4},{4,6},{6,8},{8,10},{10,12},{12,14},{14,0},{1,3},{3,5},... | collective-permute-start | bytes 1572872 | tf_op jit(solution)/shard_map/ppermute | solution.py:232
  145.3 13.9 %collective-permute-start.34 = (bf16[512,512]{1,0:T(8,128)(2,1)S(1)}, bf16[512,512]{1,0:T(8,128)(2,1)S(1)}, u32[]{:S(2)}, u32[]{:S(2)}) collective-permute-start(bf16[512,512]{1,0:T(8,128)(2,1)S(1)} %add_convert_fusion.3), channel_id=1, source_target_pairs={{0,14},{2,0},{4,2},{6,4},{8,6},{10,8},{12,10},{14,12},{1,15},{3,1}... | collective-permute-start | bytes 1572872 | tf_op jit(solution)/shard_map/ppermute | solution.py:235
  158.8 13.8 %collective-permute-start.31 = (bf16[512,512]{1,0:T(8,128)(2,1)S(1)}, bf16[512,512]{1,0:T(8,128)(2,1)S(1)}, u32[]{:S(2)}, u32[]{:S(2)}) collective-permute-start(bf16[512,512]{1,0:T(8,128)(2,1)S(1)} %add_convert_fusion.5), channel_id=1, source_target_pairs={{0,2},{2,4},{4,6},{6,8},{8,10},{10,12},{12,14},{14,0},{1,3},{3,5},... | collective-permute-start | bytes 1572872 | tf_op jit(solution)/shard_map/ppermute | solution.py:232
  159.3 13.5 %collective-permute-start.35 = (bf16[512,512]{1,0:T(8,128)(2,1)S(1)}, bf16[512,512]{1,0:T(8,128)(2,1)S(1)}, u32[]{:S(2)}, u32[]{:S(2)}) collective-permute-start(bf16[512,512]{1,0:T(8,128)(2,1)S(1)} %add_convert_fusion.2), channel_id=1, source_target_pairs={{0,14},{2,0},{4,2},{6,4},{8,6},{10,8},{12,10},{14,12},{1,15},{3,1}... | collective-permute-start | bytes 1572872 | tf_op jit(solution)/shard_map/ppermute | solution.py:235
  172.7 12.9 %collective-permute-start.32 = (bf16[512,512]{1,0:T(8,128)(2,1)S(1)}, bf16[512,512]{1,0:T(8,128)(2,1)S(1)}, u32[]{:S(2)}, u32[]{:S(2)}) collective-permute-start(bf16[512,512]{1,0:T(8,128)(2,1)S(1)} %add_convert_fusion.4), channel_id=1, source_target_pairs={{0,2},{2,4},{4,6},{6,8},{8,10},{10,12},{12,14},{14,0},{1,3},{3,5},... | collective-permute-start | bytes 1572872 | tf_op jit(solution)/shard_map/ppermute | solution.py:232
  173.0 12.6 %collective-permute-start.36 = (bf16[512,512]{1,0:T(8,128)(2,1)S(1)}, bf16[512,512]{1,0:T(8,128)(2,1)S(1)}, u32[]{:S(2)}, u32[]{:S(2)}) collective-permute-start(bf16[512,512]{1,0:T(8,128)(2,1)S(1)} %add_convert_fusion.1), channel_id=1, source_target_pairs={{0,14},{2,0},{4,2},{6,4},{8,6},{10,8},{12,10},{14,12},{1,15},{3,1}... | collective-permute-start | bytes 1572872 | tf_op jit(solution)/shard_map/ppermute | solution.py:235
  (47 other events, 708.0 us)

commit v3 on v2

--- a/solution.py
+++ b/solution.py
@@ -54,8 +54,8 @@
 
     def peer_step(g, _):
         total = None
-        for j in range(GROUP):
-            term = jnp.dot(rows[GROUP * g + j], peer_rows[GROUP * g + j], preferred_element_type=F32)
+        for j in range(2 * GROUP):
+            term = jnp.dot(rows[2 * GROUP * g + j], peer_rows[2 * GROUP * g + j], preferred_element_type=F32)
             total = term if total is None else total + term
         peer_sums[...] += total
         return 0
@@ -64,7 +64,7 @@
     peer_sums[...] = jnp.zeros(peer_sums.shape, F32)
     lax.fori_loop(0, n_chunks // GROUP, own_step, 0)
     pltpu.make_async_copy(peer_rows, peer_rows, sems.at[2 * n_chunks]).wait()
-    lax.fori_loop(0, n_chunks // GROUP, peer_step, 0)
+    lax.fori_loop(0, n_chunks // (2 * GROUP), peer_step, 0)
     for half, sums in enumerate((own_sums, peer_sums)):
         keys, values = sums[:, :width].astype(BF16), sums[:, width : 2 * width].astype(BF16)
         product = (keys.astype(F32) * values.astype(F32)).astype(BF16)
@@ -84,7 +84,7 @@
             return tuple(f * s + now for f, s in zip(falls, states))
 
         states = lax.fori_loop(
-            0, steps, step, tuple(jnp.zeros((SEGS, 128), F32) for _ in range(ORDER)), unroll=4
+            0, steps, step, tuple(jnp.zeros((SEGS, 128), F32) for _ in range(ORDER)), unroll=8
         )
         for n in range(ORDER):
             ends[n, :, lanes] = states[n]

time: 195 us -> 195 us (level)
  transfers between devices with their start and end apart: 38 -> 38, of which waited for: 20 -> 19; matrix products, arithmetic and copies ran while one was open for 7% -> 7% of each run, Pallas kernels for 19% -> 18%
where the time goes in v3:
time: 195 us
  waiting for transfers between devices  73.5 us (38%)
  starting transfers between devices  59.8 us (31%)
  Pallas kernels  39.6 us (20%)
  local copies, waits for them, and re-layouts  13.7 us (7%)
  other arithmetic  7.44 us (4%)
    ppermute x11, waiting for transfers between devices, ahead_z(): return lax.ppermute(x, 'z', around(n_z, 1))  46.5 us
    ppermute x11, starting transfers between devices, back_z(): return lax.ppermute(x, 'z', around(n_z, -1))  33.6 us
    ppermute x9, waiting for transfers between devices, swap(): return lax.ppermute(piece, axis, SWAP)  20.3 us
    pallas_call x1, Pallas kernels, per_device(): pl.pallas_call(lambda *refs: project_all(*refs, n_chunks=len(chunks)), in...  13.3 us
    ppermute x9, starting transfers between devices, swap(): return lax.ppermute(piece, axis, SWAP)  12.2 us
    pallas_call x2, Pallas kernels, project_cols(): pl.pallas_call(lambda *refs: project_out(*refs, first=first, n_parts=len(...  11.5 us
    pallas_call x1, Pallas kernels, per_device(): pl.pallas_call(lambda *refs: convolve(*refs, n_given=len(given)), in_spec...  7.17 us
    ppermute x11, starting transfers between devices, ahead_z(): return lax.ppermute(x, 'z', around(n_z, 1))  5.89 us
  transfers between devices with their start and end apart: 38, of which 19 were waited for; matrix products, arithmetic and copies ran while one was open for 7% of the time, Pallas kernels for 18%

profile of v3, /device:TPU:8, one launch (start us, length us, event | category | flops | bytes accessed | tf_op | source)
XLA Modules:
  0.0 194.6 jit_solution(16303005122039368947)
XLA Ops:
  3.1 4.0 %collective-permute-start.1 = (bf16[512,256]{1,0:T(8,128)(2,1)S(1)}, bf16[512,256]{1,0:T(8,128)(2,1)S(1)}, u32[]{:S(2)}, u32[]{:S(2)}) collective-permute-start(bf16[512,256]{1,0:T(8,128)(2,1)S(1)} %get-tuple-element.106.refs_1_), channel_id=1, source_target_pairs={{0,14},{2,0},{4,2},{6,4},{8,6},{10,8},{12,10},{14,12},{1,15},{3,1}... | collective-permute-start | bytes 786440 | tf_op jit(solution)/shard_map/ppermute | solution.py:235
  7.1 3.0 %collective-permute-start.2 = (bf16[512,256]{1,0:T(8,128)(2,1)S(1)}, bf16[512,256]{1,0:T(8,128)(2,1)S(1)}, u32[]{:S(2)}, u32[]{:S(2)}) collective-permute-start(bf16[512,256]{1,0:T(8,128)(2,1)S(1)} %get-tuple-element.105), channel_id=1, source_target_pairs={{0,1},{1,0},{2,3},{3,2},{4,5},{5,4},{6,7},{7,6},{8,9},{9,8},{10,11... | collective-permute-start | bytes 786440 | tf_op jit(solution)/shard_map/ppermute | solution.py:227
  13.2 4.1 %collective-permute-done.3 = f32[33,256]{1,0:T(8,128)S(1)} collective-permute-done((f32[33,256]{1,0:T(8,128)S(1)}, f32[33,256]{1,0:T(8,128)S(1)}, u32[]{:S(2)}, u32[]{:S(2)}) %collective-permute-start.3) | collective-permute-done | bytes 33824 | tf_op jit(solution)/shard_map/ppermute | solution.py:227
  17.3 3.1 %collective-permute-start.16 = (bf16[2,8,256,256]{3,2,1,0:T(8,128)(2,1)S(1)}, bf16[2,8,256,256]{3,2,1,0:T(8,128)(2,1)}, u32[]{:S(2)}, u32[]{:S(2)}) collective-permute-start(bf16[2,8,256,256]{3,2,1,0:T(8,128)(2,1)S(1)} %bitcast.47), channel_id=1, source_target_pairs={{0,1},{1,0},{2,3},{3,2},{4,5},{5,4},{6,7},{7,6},{8,9},{9,8},{10,11... | collective-permute-start | bytes 6291464 | tf_op jit(solution)/shard_map/ppermute | solution.py:227
  20.8 3.2 %collective-permute-start.7 = (bf16[512,256]{1,0:T(8,128)(2,1)S(1)}, bf16[512,256]{1,0:T(8,128)(2,1)S(1)}, u32[]{:S(2)}, u32[]{:S(2)}) collective-permute-start(bf16[512,256]{1,0:T(8,128)(2,1)S(1)} %collective-permute-done.2.refs_9_), channel_id=1, source_target_pairs={{0,14},{2,0},{4,2},{6,4},{8,6},{10,8},{12,10},{14,12},{1,15},{3,1}... | collective-permute-start | bytes 786440 | tf_op jit(solution)/shard_map/ppermute | solution.py:235
  24.1 3.2 %collective-permute-start.5 = (bf16[512,256]{1,0:T(8,128)(2,1)S(1)}, bf16[512,256]{1,0:T(8,128)(2,1)}, u32[]{:S(2)}, u32[]{:S(2)}) collective-permute-start(bf16[512,256]{1,0:T(8,128)(2,1)S(1)} %collective-permute-done.1.refs_6_), channel_id=1, source_target_pairs={{0,14},{2,0},{4,2},{6,4},{8,6},{10,8},{12,10},{14,12},{1,15},{3,1}... | collective-permute-start | bytes 786440 | tf_op jit(solution)/shard_map/ppermute | solution.py:235
  29.6 4.7 %collective-permute-done.4.refs_3_ = bf16[512,256]{1,0:T(8,128)(2,1)} collective-permute-done((bf16[512,256]{1,0:T(8,128)(2,1)S(1)}, bf16[512,256]{1,0:T(8,128)(2,1)}, u32[]{:S(2)}, u32[]{:S(2)}) %collective-permute-start.4) | collective-permute-done | bytes 262176 | tf_op jit(solution)/shard_map/ppermute | solution.py:232
  34.5 3.2 %collective-permute-start.11 = (bf16[512,256]{1,0:T(8,128)(2,1)S(1)}, bf16[512,256]{1,0:T(8,128)(2,1)S(1)}, u32[]{:S(2)}, u32[]{:S(2)}) collective-permute-start(bf16[512,256]{1,0:T(8,128)(2,1)S(1)} %collective-permute-done.7.refs_13_), channel_id=1, source_target_pairs={{0,14},{2,0},{4,2},{6,4},{8,6},{10,8},{12,10},{14,12},{1,15},{3,1}... | collective-permute-start | bytes 786440 | tf_op jit(solution)/shard_map/ppermute | solution.py:235
  37.7 3.2 %collective-permute-start.9 = (bf16[512,256]{1,0:T(8,128)(2,1)}, bf16[512,256]{1,0:T(8,128)(2,1)S(1)}, u32[]{:S(2)}, u32[]{:S(2)}) collective-permute-start(bf16[512,256]{1,0:T(8,128)(2,1)} %collective-permute-done.5.refs_7_), channel_id=1, source_target_pairs={{0,14},{2,0},{4,2},{6,4},{8,6},{10,8},{12,10},{14,12},{1,15},{3,1}... | collective-permute-start | bytes 786440 | tf_op jit(solution)/shard_map/ppermute | solution.py:235
  40.9 3.3 %collective-permute-done.10.refs_11_ = bf16[512,256]{1,0:T(8,128)(2,1)S(1)} collective-permute-done((bf16[512,256]{1,0:T(8,128)(2,1)S(1)}, bf16[512,256]{1,0:T(8,128)(2,1)S(1)}, u32[]{:S(2)}, u32[]{:S(2)}) %collective-permute-start.10) | collective-permute-done | bytes 262176 | tf_op jit(solution)/shard_map/ppermute | solution.py:232
  51.7 4.5 %collective-permute-done.12.refs_5_ = bf16[512,256]{1,0:T(8,128)(2,1)S(1)} collective-permute-done((bf16[512,256]{1,0:T(8,128)(2,1)S(1)}, bf16[512,256]{1,0:T(8,128)(2,1)S(1)}, u32[]{:S(2)}, u32[]{:S(2)}) %collective-permute-start.12) | collective-permute-done | bytes 262176 | tf_op jit(solution)/shard_map/ppermute | solution.py:232
  72.1 13.3 %shard_map.73 = (bf16[512,512]{1,0:T(8,128)(2,1)}, f32[16,8,512]{2,1,0:T(8,128)}, f32[16,512]{1,0:T(8,128)}, bf16[512,256]{1,0:T(8,128)(2,1)}) custom-call(s32[18]{0:T(128)} %stack.159.refs_0_, bf16[512,256]{1,0:T(8,128)(2,1)} %copy-done.3, bf16[512,256]{1,0:T(8,128)(2,1)} %copy-done.5, bf16[512,256]{1,0:T(8,128)(2,1)} %collective-permute-done.4.refs_3_, ...), custom_call_target="tpu_custom_call" | custom-call | tf_op jit(solution)/shard_map/pallas_call | solution.py:280
  106.7 5.9 %shard_map.75.refs_7_ = bf16[512,256]{1,0:T(8,128)(2,1)} custom-call(s32[18]{0:T(128)} %stack.159.refs_0_, bf16[512,256]{1,0:T(8,128)(2,1)} %copy-done.3, bf16[512,256]{1,0:T(8,128)(2,1)} %copy-done.5, bf16[512,256]{1,0:T(8,128)(2,1)} %collective-permute-done.4.refs_3_, bf16[512,256]{1,0:T(8,128)(2,1)} %copy-done.12, bf16[512,256]{1,0:T(8,128)(2,1)} %copy-done.14, ...), custom_call_target="tpu_custom_call" | custom-call | tf_op jit(solution)/shard_map/pallas_call | solution.py:312
  113.2 7.2 %shard_map.76.refs_1_ = bf16[512,512]{1,0:T(8,128)(2,1)} custom-call(f32[16,512]{1,0:T(8,128)} %get-tuple-element.84.refs_0_, f32[16,512]{1,0:T(8,128)} %copy-done.28, f32[16,512]{1,0:T(8,128)} %copy-done.29, f32[16,512]{1,0:T(8,128)} %copy-done.30, f32[16,8,512]{2,1,0:T(8,128)} %get-tuple-element.88.refs_4_, bf16[512,512]{1,0:T(8,128)(2,1)} %get-tuple-element.89.refs_5_, ...), custom_call_target="tpu_custom_call" | custom-call | tf_op jit(solution)/shard_map/pallas_call | solution.py:332
  120.4 3.8 %collective-permute-done.23.refs_3_ = bf16[256,2048]{1,0:T(8,128)(2,1)S(1)} collective-permute-done((bf16[256,2048]{1,0:T(8,128)(2,1)S(1)}, bf16[256,2048]{1,0:T(8,128)(2,1)S(1)}, u32[]{:S(2)}, u32[]{:S(2)}) %collective-permute-start.23) | collective-permute-done | bytes 1048608 | tf_op jit(solution)/shard_map/ppermute | solution.py:227
  127.8 3.9 %shard_map.77 = (bf16[256,512]{1,0:T(8,128)(2,1)}, bf16[256,512]{1,0:T(8,128)(2,1)}) custom-call(s32[10]{0:T(128)} %stack.170.refs_0_, bf16[512,512]{1,0:T(8,128)(2,1)} %shard_map.76.refs_1_, bf16[256,4096]{1,0:T(8,128)(2,1)} %refs_2_.3, bf16[256,2048]{1,0:T(8,128)(2,1)} %copy-done.1, bf16[256,2048]{1,0:T(8,128)(2,1)} %copy-done.2), custom_call_target="tpu_custom_call" | custom-call | tf_op jit(solution)/shard_map/pallas_call | solution.py:344
  135.1 7.5 %shard_map.78 = (bf16[512,512]{1,0:T(8,128)(2,1)}, bf16[512,512]{1,0:T(8,128)(2,1)}, bf16[512,512]{1,0:T(8,128)(2,1)}, bf16[512,512]{1,0:T(8,128)(2,1)}, bf16[51...) custom-call(s32[10]{0:T(128)} %stack.170.refs_0_, bf16[512,512]{1,0:T(8,128)(2,1)} %shard_map.76.refs_1_, ...), custom_call_target="tpu_custom_call" | custom-call | tf_op jit(solution)/shard_map/pallas_call | solution.py:344
  145.1 3.3 %collective-permute-start.34 = (bf16[512,512]{1,0:T(8,128)(2,1)S(1)}, bf16[512,512]{1,0:T(8,128)(2,1)S(1)}, u32[]{:S(2)}, u32[]{:S(2)}) collective-permute-start(bf16[512,512]{1,0:T(8,128)(2,1)S(1)} %add_convert_fusion.3), channel_id=1, source_target_pairs={{0,14},{2,0},{4,2},{6,4},{8,6},{10,8},{12,10},{14,12},{1,15},{3,1}... | collective-permute-start | bytes 1572872 | tf_op jit(solution)/shard_map/ppermute | solution.py:235
  148.4 10.1 %collective-permute-done.30 = bf16[512,512]{1,0:T(8,128)(2,1)S(1)} collective-permute-done((bf16[512,512]{1,0:T(8,128)(2,1)S(1)}, bf16[512,512]{1,0:T(8,128)(2,1)S(1)}, u32[]{:S(2)}, u32[]{:S(2)}) %collective-permute-start.30) | collective-permute-done | bytes 524320 | tf_op jit(solution)/shard_map/ppermute | solution.py:232
  159.2 3.8 %collective-permute-start.35 = (bf16[512,512]{1,0:T(8,128)(2,1)S(1)}, bf16[512,512]{1,0:T(8,128)(2,1)S(1)}, u32[]{:S(2)}, u32[]{:S(2)}) collective-permute-start(bf16[512,512]{1,0:T(8,128)(2,1)S(1)} %add_convert_fusion.2), channel_id=1, source_target_pairs={{0,14},{2,0},{4,2},{6,4},{8,6},{10,8},{12,10},{14,12},{1,15},{3,1}... | collective-permute-start | bytes 1572872 | tf_op jit(solution)/shard_map/ppermute | solution.py:235
  163.0 9.5 %collective-permute-done.31 = bf16[512,512]{1,0:T(8,128)(2,1)S(1)} collective-permute-done((bf16[512,512]{1,0:T(8,128)(2,1)S(1)}, bf16[512,512]{1,0:T(8,128)(2,1)S(1)}, u32[]{:S(2)}, u32[]{:S(2)}) %collective-permute-start.31) | collective-permute-done | bytes 524320 | tf_op jit(solution)/shard_map/ppermute | solution.py:232
  172.9 3.7 %collective-permute-start.36 = (bf16[512,512]{1,0:T(8,128)(2,1)S(1)}, bf16[512,512]{1,0:T(8,128)(2,1)S(1)}, u32[]{:S(2)}, u32[]{:S(2)}) collective-permute-start(bf16[512,512]{1,0:T(8,128)(2,1)S(1)} %add_convert_fusion.1), channel_id=1, source_target_pairs={{0,14},{2,0},{4,2},{6,4},{8,6},{10,8},{12,10},{14,12},{1,15},{3,1}... | collective-permute-start | bytes 1572872 | tf_op jit(solution)/shard_map/ppermute | solution.py:235
  176.6 8.9 %collective-permute-done.32 = bf16[512,512]{1,0:T(8,128)(2,1)S(1)} collective-permute-done((bf16[512,512]{1,0:T(8,128)(2,1)S(1)}, bf16[512,512]{1,0:T(8,128)(2,1)S(1)}, u32[]{:S(2)}, u32[]{:S(2)}) %collective-permute-start.32) | collective-permute-done | bytes 524320 | tf_op jit(solution)/shard_map/ppermute | solution.py:232
  187.6 6.0 %collective-permute-done.37 = bf16[512,256]{1,0:T(8,128)(2,1)S(1)} collective-permute-done((bf16[512,256]{1,0:T(8,128)(2,1)S(1)}, bf16[512,256]{1,0:T(8,128)(2,1)S(1)}, u32[]{:S(2)}, u32[]{:S(2)}) %collective-permute-start.37) | collective-permute-done | bytes 262176 | tf_op jit(solution)/shard_map/ppermute | solution.py:227
  (154 shorter events, 67.5 us)
Async XLA Ops:
  1.1 16.2 %collective-permute-start = (bf16[512,256]{1,0:T(8,128)(2,1)S(1)}, bf16[512,256]{1,0:T(8,128)(2,1)S(1)}, u32[]{:S(2)}, u32[]{:S(2)}) collective-permute-start(bf16[512,256]{1,0:T(8,128)(2,1)S(1)} %get-tuple-element.106.refs_1_), channel_id=1, source_target_pairs={{0,2},{2,4},{4,6},{6,8},{8,10},{10,12},{12,14},{14,0},{1,3},{3,5},... | collective-permute-start | bytes 786440 | tf_op jit(solution)/shard_map/ppermute | solution.py:232
  3.1 14.2 %collective-permute-start.1 = (bf16[512,256]{1,0:T(8,128)(2,1)S(1)}, bf16[512,256]{1,0:T(8,128)(2,1)S(1)}, u32[]{:S(2)}, u32[]{:S(2)}) collective-permute-start(bf16[512,256]{1,0:T(8,128)(2,1)S(1)} %get-tuple-element.106.refs_1_), channel_id=1, source_target_pairs={{0,14},{2,0},{4,2},{6,4},{8,6},{10,8},{12,10},{14,12},{1,15},{3,1}... | collective-permute-start | bytes 786440 | tf_op jit(solution)/shard_map/ppermute | solution.py:235
  7.1 10.2 %collective-permute-start.2 = (bf16[512,256]{1,0:T(8,128)(2,1)S(1)}, bf16[512,256]{1,0:T(8,128)(2,1)S(1)}, u32[]{:S(2)}, u32[]{:S(2)}) collective-permute-start(bf16[512,256]{1,0:T(8,128)(2,1)S(1)} %get-tuple-element.105), channel_id=1, source_target_pairs={{0,1},{1,0},{2,3},{3,2},{4,5},{5,4},{6,7},{7,6},{8,9},{9,8},{10,11... | collective-permute-start | bytes 786440 | tf_op jit(solution)/shard_map/ppermute | solution.py:227
  17.3 49.1 %collective-permute-start.16 = (bf16[2,8,256,256]{3,2,1,0:T(8,128)(2,1)S(1)}, bf16[2,8,256,256]{3,2,1,0:T(8,128)(2,1)}, u32[]{:S(2)}, u32[]{:S(2)}) collective-permute-start(bf16[2,8,256,256]{3,2,1,0:T(8,128)(2,1)S(1)} %bitcast.47), channel_id=1, source_target_pairs={{0,1},{1,0},{2,3},{3,2},{4,5},{5,4},{6,7},{7,6},{8,9},{9,8},{10,11... | collective-permute-start | bytes 6291464 | tf_op jit(solution)/shard_map/ppermute | solution.py:227
  20.8 13.6 %collective-permute-start.6 = (bf16[512,256]{1,0:T(8,128)(2,1)S(1)}, bf16[512,256]{1,0:T(8,128)(2,1)S(1)}, u32[]{:S(2)}, u32[]{:S(2)}) collective-permute-start(bf16[512,256]{1,0:T(8,128)(2,1)S(1)} %collective-permute-done.2.refs_9_), channel_id=1, source_target_pairs={{0,2},{2,4},{4,6},{6,8},{8,10},{10,12},{12,14},{14,0},{1,3},{3,5},... | collective-permute-start | bytes 786440 | tf_op jit(solution)/shard_map/ppermute | solution.py:232
  20.8 13.5 %collective-permute-start.7 = (bf16[512,256]{1,0:T(8,128)(2,1)S(1)}, bf16[512,256]{1,0:T(8,128)(2,1)S(1)}, u32[]{:S(2)}, u32[]{:S(2)}) collective-permute-start(bf16[512,256]{1,0:T(8,128)(2,1)S(1)} %collective-permute-done.2.refs_9_), channel_id=1, source_target_pairs={{0,14},{2,0},{4,2},{6,4},{8,6},{10,8},{12,10},{14,12},{1,15},{3,1}... | collective-permute-start | bytes 786440 | tf_op jit(solution)/shard_map/ppermute | solution.py:235
  24.1 10.3 %collective-permute-start.4 = (bf16[512,256]{1,0:T(8,128)(2,1)S(1)}, bf16[512,256]{1,0:T(8,128)(2,1)}, u32[]{:S(2)}, u32[]{:S(2)}) collective-permute-start(bf16[512,256]{1,0:T(8,128)(2,1)S(1)} %collective-permute-done.refs_2_), channel_id=1, source_target_pairs={{0,2},{2,4},{4,6},{6,8},{8,10},{10,12},{12,14},{14,0},{1,3},{3,5},... | collective-permute-start | bytes 786440 | tf_op jit(solution)/shard_map/ppermute | solution.py:232
  24.1 10.3 %collective-permute-start.5 = (bf16[512,256]{1,0:T(8,128)(2,1)S(1)}, bf16[512,256]{1,0:T(8,128)(2,1)}, u32[]{:S(2)}, u32[]{:S(2)}) collective-permute-start(bf16[512,256]{1,0:T(8,128)(2,1)S(1)} %collective-permute-done.1.refs_6_), channel_id=1, source_target_pairs={{0,14},{2,0},{4,2},{6,4},{8,6},{10,8},{12,10},{14,12},{1,15},{3,1}... | collective-permute-start | bytes 786440 | tf_op jit(solution)/shard_map/ppermute | solution.py:235
  34.4 9.8 %collective-permute-start.10 = (bf16[512,256]{1,0:T(8,128)(2,1)S(1)}, bf16[512,256]{1,0:T(8,128)(2,1)S(1)}, u32[]{:S(2)}, u32[]{:S(2)}) collective-permute-start(bf16[512,256]{1,0:T(8,128)(2,1)S(1)} %collective-permute-done.6.refs_10_), channel_id=1, source_target_pairs={{0,2},{2,4},{4,6},{6,8},{8,10},{10,12},{12,14},{14,0},{1,3},{3,5},... | collective-permute-start | bytes 786440 | tf_op jit(solution)/shard_map/ppermute | solution.py:232
  34.5 9.7 %collective-permute-start.11 = (bf16[512,256]{1,0:T(8,128)(2,1)S(1)}, bf16[512,256]{1,0:T(8,128)(2,1)S(1)}, u32[]{:S(2)}, u32[]{:S(2)}) collective-permute-start(bf16[512,256]{1,0:T(8,128)(2,1)S(1)} %collective-permute-done.7.refs_13_), channel_id=1, source_target_pairs={{0,14},{2,0},{4,2},{6,4},{8,6},{10,8},{12,10},{14,12},{1,15},{3,1}... | collective-permute-start | bytes 786440 | tf_op jit(solution)/shard_map/ppermute | solution.py:235
  48.4 10.5 %collective-permute-start.13 = (bf16[512,256]{1,0:T(8,128)(2,1)S(1)}, bf16[512,256]{1,0:T(8,128)(2,1)S(1)}, u32[]{:S(2)}, u32[]{:S(2)}) collective-permute-start(bf16[512,256]{1,0:T(8,128)(2,1)S(1)} %collective-permute-done.10.refs_11_), channel_id=1, source_target_pairs={{0,2},{2,4},{4,6},{6,8},{8,10},{10,12},{12,14},{14,0},{1,3},{3,5},... | collective-permute-start | bytes 786440 | tf_op jit(solution)/shard_map/ppermute | solution.py:232
  66.4 27.9 %collective-permute-start.17 = (bf16[1,8,256,256]{3,2,1,0:T(8,128)(2,1)}, bf16[1,8,256,256]{3,2,1,0:T(8,128)(2,1)}, u32[]{:S(2)}, u32[]{:S(2)}) collective-permute-start(bf16[1,8,256,256]{3,2,1,0:T(8,128)(2,1)} %bitcast.44), channel_id=1, source_target_pairs={{0,1},{1,0},{2,3},{3,2},{4,5},{5,4},{6,7},{7,6},{8,9},{9,8},{10,11... | collective-permute-start | bytes 3145736 | tf_op jit(solution)/shard_map/ppermute | solution.py:227
  97.1 27.1 %collective-permute-start.23 = (bf16[256,2048]{1,0:T(8,128)(2,1)S(1)}, bf16[256,2048]{1,0:T(8,128)(2,1)S(1)}, u32[]{:S(2)}, u32[]{:S(2)}) collective-permute-start(bf16[256,2048]{1,0:T(8,128)(2,1)S(1)} %constant_dynamic-slice_fusion.1), channel_id=1, source_target_pairs={{0,1},{1,0},{2,3},{3,2},{4,5},{5,4},{6,7},{7,6},{8,9},{9,8},{10,11... | collective-permute-start | bytes 3145736 | tf_op jit(solution)/shard_map/ppermute | solution.py:227
  100.7 11.8 %collective-permute-start.24 = (f32[16,512]{1,0:T(8,128)}, f32[16,512]{1,0:T(8,128)S(1)}, u32[]{:S(2)}, u32[]{:S(2)}) collective-permute-start(f32[16,512]{1,0:T(8,128)} %get-tuple-element.85), channel_id=1, source_target_pairs={{0,64},{64,128},{128,192},{192,0},{1,65},{65,129},{129,193},{193,1... | collective-permute-start | bytes 98312 | tf_op jit(solution)/shard_map/ppermute | solution.py:330
  102.3 10.3 %collective-permute-start.25 = (f32[16,512]{1,0:T(8,128)}, f32[16,512]{1,0:T(8,128)S(1)}, u32[]{:S(2)}, u32[]{:S(2)}) collective-permute-start(f32[16,512]{1,0:T(8,128)} %get-tuple-element.86), channel_id=1, source_target_pairs={{0,192},{64,0},{128,64},{192,128},{1,193},{65,1},{129,65},{193,129... | collective-permute-start | bytes 98312 | tf_op jit(solution)/shard_map/ppermute | solution.py:330
  102.8 9.8 %collective-permute-start.26 = (f32[16,512]{1,0:T(8,128)}, f32[16,512]{1,0:T(8,128)S(1)}, u32[]{:S(2)}, u32[]{:S(2)}) collective-permute-start(f32[16,512]{1,0:T(8,128)} %get-tuple-element.87), channel_id=1, source_target_pairs={{0,128},{64,192},{128,0},{192,64},{1,129},{65,193},{129,1},{193,65... | collective-permute-start | bytes 98312 | tf_op jit(solution)/shard_map/ppermute | solution.py:330
  131.8 10.8 %collective-permute-start.29 = (bf16[256,512]{1,0:T(8,128)(2,1)}, bf16[256,512]{1,0:T(8,128)(2,1)S(1)}, u32[]{:S(2)}, u32[]{:S(2)}) collective-permute-start(bf16[256,512]{1,0:T(8,128)(2,1)} %get-tuple-element.94), channel_id=1, source_target_pairs={{0,2},{2,4},{4,6},{6,8},{8,10},{10,12},{12,14},{14,0},{1,3},{3,5},... | collective-permute-start | bytes 786440 | tf_op jit(solution)/shard_map/ppermute | solution.py:232
  132.1 11.8 %collective-permute-start.33 = (bf16[256,512]{1,0:T(8,128)(2,1)}, bf16[256,512]{1,0:T(8,128)(2,1)S(1)}, u32[]{:S(2)}, u32[]{:S(2)}) collective-permute-start(bf16[256,512]{1,0:T(8,128)(2,1)} %get-tuple-element.98), channel_id=1, source_target_pairs={{0,14},{2,0},{4,2},{6,4},{8,6},{10,8},{12,10},{14,12},{1,15},{3,1}... | collective-permute-start | bytes 786440 | tf_op jit(solution)/shard_map/ppermute | solution.py:235
  143.9 14.7 %collective-permute-start.30 = (bf16[512,512]{1,0:T(8,128)(2,1)S(1)}, bf16[512,512]{1,0:T(8,128)(2,1)S(1)}, u32[]{:S(2)}, u32[]{:S(2)}) collective-permute-start(bf16[512,512]{1,0:T(8,128)(2,1)S(1)} %add_convert_fusion.6), channel_id=1, source_target_pairs={{0,2},{2,4},{4,6},{6,8},{8,10},{10,12},{12,14},{14,0},{1,3},{3,5},... | collective-permute-start | bytes 1572872 | tf_op jit(solution)/shard_map/ppermute | solution.py:232
  145.1 13.9 %collective-permute-start.34 = (bf16[512,512]{1,0:T(8,128)(2,1)S(1)}, bf16[512,512]{1,0:T(8,128)(2,1)S(1)}, u32[]{:S(2)}, u32[]{:S(2)}) collective-permute-start(bf16[512,512]{1,0:T(8,128)(2,1)S(1)} %add_convert_fusion.3), channel_id=1, source_target_pairs={{0,14},{2,0},{4,2},{6,4},{8,6},{10,8},{12,10},{14,12},{1,15},{3,1}... | collective-permute-start | bytes 1572872 | tf_op jit(solution)/shard_map/ppermute | solution.py:235
  158.7 13.8 %collective-permute-start.31 = (bf16[512,512]{1,0:T(8,128)(2,1)S(1)}, bf16[512,512]{1,0:T(8,128)(2,1)S(1)}, u32[]{:S(2)}, u32[]{:S(2)}) collective-permute-start(bf16[512,512]{1,0:T(8,128)(2,1)S(1)} %add_convert_fusion.5), channel_id=1, source_target_pairs={{0,2},{2,4},{4,6},{6,8},{8,10},{10,12},{12,14},{14,0},{1,3},{3,5},... | collective-permute-start | bytes 1572872 | tf_op jit(solution)/shard_map/ppermute | solution.py:232
  159.2 13.5 %collective-permute-start.35 = (bf16[512,512]{1,0:T(8,128)(2,1)S(1)}, bf16[512,512]{1,0:T(8,128)(2,1)S(1)}, u32[]{:S(2)}, u32[]{:S(2)}) collective-permute-start(bf16[512,512]{1,0:T(8,128)(2,1)S(1)} %add_convert_fusion.2), channel_id=1, source_target_pairs={{0,14},{2,0},{4,2},{6,4},{8,6},{10,8},{12,10},{14,12},{1,15},{3,1}... | collective-permute-start | bytes 1572872 | tf_op jit(solution)/shard_map/ppermute | solution.py:235
  172.6 12.9 %collective-permute-start.32 = (bf16[512,512]{1,0:T(8,128)(2,1)S(1)}, bf16[512,512]{1,0:T(8,128)(2,1)S(1)}, u32[]{:S(2)}, u32[]{:S(2)}) collective-permute-start(bf16[512,512]{1,0:T(8,128)(2,1)S(1)} %add_convert_fusion.4), channel_id=1, source_target_pairs={{0,2},{2,4},{4,6},{6,8},{8,10},{10,12},{12,14},{14,0},{1,3},{3,5},... | collective-permute-start | bytes 1572872 | tf_op jit(solution)/shard_map/ppermute | solution.py:232
  172.9 12.6 %collective-permute-start.36 = (bf16[512,512]{1,0:T(8,128)(2,1)S(1)}, bf16[512,512]{1,0:T(8,128)(2,1)S(1)}, u32[]{:S(2)}, u32[]{:S(2)}) collective-permute-start(bf16[512,512]{1,0:T(8,128)(2,1)S(1)} %add_convert_fusion.1), channel_id=1, source_target_pairs={{0,14},{2,0},{4,2},{6,4},{8,6},{10,8},{12,10},{14,12},{1,15},{3,1}... | collective-permute-start | bytes 1572872 | tf_op jit(solution)/shard_map/ppermute | solution.py:235
  (47 other events, 709.9 us)
